TPU v7x, 32 devices: a whole 2x2x4 slice. The times are simulated.
32 devices in a mesh: shot: 4 (over y, x), dom: 8 (over z, core).
Axes of the slice: x: 2, y: 2, z: 4, core: 2. Of those that a mesh axis runs over, the one named last changes fastest.
Arguments:
- velocity: float32 [256, 32, 128], P('dom'), may hold values from 1.5 to 3
- noise_field: float32 [256, 32, 128], P('dom'), may hold values from -6 to 6
- step_size: float32 [1], replicated, may hold values from 0.05 to 0.5
- field_prev: float32 [8, 256, 32, 128], P('shot', 'dom'), may hold values from -6 to 6
- field_now: float32 [8, 256, 32, 128], P('shot', 'dom'), may hold values from -6 to 6
- adjoint_next: float32 [8, 256, 32, 128], P('shot', 'dom'), may hold values from -6 to 6
- adjoint_now: float32 [8, 256, 32, 128], P('shot', 'dom'), may hold values from -6 to 6
- wavelet: float32 [8, 4], P('shot'), may hold values from -8 to 8
- source_cells: int32 [8, 8], P('shot'), may hold values from 0 to 1048575
- source_signs: int32 [8, 8], P('shot'), may hold values from 0 to 1
- record_cells: int32 [8, 256], P('shot'), may hold values from 0 to 1048575
- observed: float32 [8, 4, 256], P('shot'), may hold values from -6 to 6
Outputs:
- new_velocity: float32 [256, 32, 128], P('dom', None, 'shot')
Inputs may be any that keep to these rules, and one draw needn't show every extreme that they name: `source_signs`: 0 stands for a negative sign, 1 for a positive one. `source_cells`: cells flattened as x 32 * 128 + z * 128 + y. `record_cells`: cells flattened as x 32 * 128 + z * 128 + y.
All inputs are finite; a program needn't handle non-finite values.
Results may differ from a plain program's by a relative error of at most 0.00009.
Values sent between devices are 32-bit elements; how exact they have to be, the bound alone decides.
A program may use at most 128 MiB of HBM per device.

v0:
```python
import functools
import math

import jax
import jax.numpy as jnp
import numpy as np
from jax import lax
from jax.experimental import pallas as pl
from jax.experimental.pallas import tpu as pltpu
from jax.sharding import PartitionSpec as P

STEPS = 4


COEFFS = (-205.0 / 72.0, 8.0 / 5.0, -1.0 / 5.0, 8.0 / 315.0, -1.0 / 560.0)
COURANT = 0.02


MARGIN = 4
MESH = pl.DeviceIdType.MESH


def split_two(value):
    high = value.astype(jnp.bfloat16)
    low = (value - high.astype(jnp.float32)).astype(jnp.bfloat16)
    return jnp.concatenate([high, low], axis=-1)


def wave_kernel(
    doms,
    now_hbm,
    adj_hbm,
    prev_hbm,
    later_hbm,
    speed_hbm,
    pulse,
    src_cells,
    src_signs,
    record_cells,
    observed,
    out,
    ext,
    prev,
    later,
    speed,
    laps,
    spread_src,
    landed,
    pick,
    put,
    hot,
    columns,
    misfit,
    total,
    load_sem,
    send_sem,
    recv_sem,
):
    shots, rows, depth, width = prev.shape
    here = lax.axis_index("dom")
    left = jnp.maximum(here - 1, 0)
    right = jnp.minimum(here + 1, doms - 1)
    has_left = here > 0
    has_right = here < doms - 1
    chunk = 8
    chunks = rows // chunk
    high_start = rows + MARGIN

    loads = [
        pltpu.make_async_copy(now_hbm, ext.at[0, :, pl.ds(MARGIN, rows)], load_sem.at[0]),
        pltpu.make_async_copy(speed_hbm, speed, load_sem.at[1]),
        pltpu.make_async_copy(prev_hbm, prev, load_sem.at[2]),
        pltpu.make_async_copy(adj_hbm, ext.at[STEPS, :, pl.ds(MARGIN, rows)], load_sem.at[3]),
        pltpu.make_async_copy(later_hbm, later, load_sem.at[4]),
    ]
    for load in loads:
        load.start()

    barrier = pltpu.get_barrier_semaphore()

    @pl.when(has_left)
    def _():
        pl.semaphore_signal(barrier, inc=1, device_id={"dom": left}, device_id_type=MESH)

    @pl.when(has_right)
    def _():
        pl.semaphore_signal(barrier, inc=1, device_id={"dom": right}, device_id_type=MESH)

    pl.semaphore_wait(barrier, has_left.astype(jnp.int32) + has_right.astype(jnp.int32))

    def halo_copies(slot, source):
        base = MARGIN if source is None else 0
        field = ext.at[slot] if source is None else source
        to_left = pltpu.make_async_remote_copy(
            src_ref=field.at[:, pl.ds(base, MARGIN)],
            dst_ref=ext.at[slot, :, pl.ds(high_start, MARGIN)],
            send_sem=send_sem.at[slot, 0],
            recv_sem=recv_sem.at[slot, 1],
            device_id={"dom": left},
            device_id_type=MESH,
        )
        to_right = pltpu.make_async_remote_copy(
            src_ref=field.at[:, pl.ds(base + rows - MARGIN, MARGIN)],
            dst_ref=ext.at[slot, :, pl.ds(0, MARGIN)],
            send_sem=send_sem.at[slot, 1],
            recv_sem=recv_sem.at[slot, 0],
            device_id={"dom": right},
            device_id_type=MESH,
        )
        return to_left, to_right

    copies = [
        halo_copies(slot, {0: now_hbm, STEPS: adj_hbm}.get(slot)) for slot in range(2 * STEPS)
    ]

    def send(slot):
        @pl.when(has_left)
        def _():
            copies[slot][0].start()

        @pl.when(has_right)
        def _():
            copies[slot][1].start()

    def receive(slot):
        @pl.when(has_left)
        def _():
            copies[slot][1].wait_recv()

        @pl.when(has_right)
        def _():
            copies[slot][0].wait_recv()

    send(0)
    send(STEPS)

    edge = jnp.zeros((2 * STEPS, shots, MARGIN, depth, width), jnp.float32)

    @pl.when(jnp.logical_not(has_left))
    def _():
        ext[pl.ds(0, 2 * STEPS), :, pl.ds(0, MARGIN)] = edge

    @pl.when(jnp.logical_not(has_right))
    def _():
        ext[pl.ds(0, 2 * STEPS), :, pl.ds(high_start, MARGIN)] = edge

    lanes = lax.broadcasted_iota(jnp.int32, (depth, width), 1)
    nothing = jnp.zeros((MARGIN, width), jnp.float32)

    span = chunk * depth
    receivers = record_cells.shape[1]
    first = here * (rows * depth)
    row_of = lambda cell: lax.div(cell, jnp.int32(width))
    lane_of = lambda cell: lax.rem(cell, jnp.int32(width))
    tile = (width, receivers)
    place = lax.broadcasted_iota(jnp.int32, tile, 0)
    for s in range(shots):
        cells = record_cells[s : s + 1, :]
        rec_rows = row_of(cells) - first
        table = jnp.where(
            place == STEPS,
            jnp.broadcast_to(rec_rows.astype(jnp.float32), tile),
            jnp.broadcast_to(lane_of(cells).astype(jnp.float32), tile),
        )
        for k in range(STEPS):
            table = jnp.where(place == k, jnp.broadcast_to(observed[s, k : k + 1, :], tile), table)
        columns[s] = jnp.transpose(table)
        rec_col = columns[s, :, STEPS : STEPS + 1].astype(jnp.int32)
        rec_lane = columns[s, :, STEPS + 1 : STEPS + 2].astype(jnp.int32)
        hot[s] = (lax.broadcasted_iota(jnp.int32, (receivers, width), 1) == rec_lane).astype(
            jnp.float32
        )
        count = src_cells.shape[1]
        padded = count + (-count) % 128
        order = lax.broadcasted_iota(jnp.int32, (padded, width), 0)
        across = lax.broadcasted_iota(jnp.int32, (padded, width), 1)
        along = lax.broadcasted_iota(jnp.int32, (1, padded), 1)
        tall = jnp.zeros((padded, width), jnp.float32)
        src_rows = jnp.full((1, padded), -1, jnp.int32)
        for j in range(count):
            cell = src_cells[s, j]
            sign = (2 * src_signs[s, j] - 1).astype(jnp.float32)
            tall = jnp.where((order == j) & (across == lane_of(cell)), sign, tall)
            src_rows = jnp.where(along == j, row_of(cell) - first, src_rows)
        tall = tall.astype(jnp.bfloat16)

        @pl.loop(0, chunks)
        def _(c):
            cell = lax.broadcasted_iota(jnp.int32, (receivers, span), 1) + c * span
            pick[s, c] = (cell == rec_col).astype(jnp.float32).astype(jnp.bfloat16)
            cell = lax.broadcasted_iota(jnp.int32, (span, receivers), 0) + c * span
            put[s, c] = (cell == rec_rows).astype(jnp.float32).astype(jnp.bfloat16)
            cell = lax.broadcasted_iota(jnp.int32, (span, padded), 0) + c * span
            wide = (cell == src_rows).astype(jnp.float32).astype(jnp.bfloat16)
            spots = jnp.dot(wide, tall, preferred_element_type=jnp.float32)
            spread_src[s, pl.ds(c * chunk, chunk)] = spots.reshape(chunk, depth, width)

    def laplacian(slot, s, x):
        middle = ext[slot, s, x + MARGIN]
        summed = 3.0 * COEFFS[0] * middle
        for r in range(1, MARGIN + 1):
            beside = ext[slot, s, x + MARGIN + r] + ext[slot, s, x + MARGIN - r]
            beside += jnp.concatenate([middle[r:], nothing[:r]], axis=0)
            beside += jnp.concatenate([nothing[:r], middle[: depth - r]], axis=0)
            beside += jnp.where(lanes < width - r, pltpu.roll(middle, width - r, 1), 0.0)
            beside += jnp.where(lanes >= r, pltpu.roll(middle, r, 1), 0.0)
            summed += COEFFS[r] * beside
        return middle, summed

    def forward(moment, first, last):
        @pl.loop(first, last, unroll=MARGIN)
        def _(x):
            squared = COURANT * speed[x] * speed[x]
            for s in range(shots):
                middle, summed = laplacian(moment, s, x)
                before = prev[s, x] if moment == 0 else ext[moment - 1, s, x + MARGIN]
                laps[moment, s, x] = summed
                slot = moment + 1 if moment + 1 < STEPS else 2 * STEPS
                ext[slot, s, x + MARGIN] = (
                    2.0 * middle - before + squared * summed + pulse[s, moment] * spread_src[s, x]
                )

    def backward(moment, first, last):
        slot = 2 * STEPS - moment

        @pl.loop(first, last, unroll=MARGIN)
        def _(x):
            squared = COURANT * speed[x] * speed[x]
            gathered = None
            for s in range(shots):
                middle, summed = laplacian(slot, s, x)
                after = later[s, x] if moment == STEPS else ext[slot - 1, s, x + MARGIN]
                earlier = 2.0 * middle - after + squared * summed + landed[moment - 1, s, x]
                if moment > 1:
                    ext[slot + 1, s, x + MARGIN] = earlier
                term = earlier * laps[moment - 1, s, x]
                gathered = term if gathered is None else gathered + term
            if moment < STEPS:
                gathered = gathered + total[x]
            if moment > 1:
                total[x] = gathered
            else:
                out[x] = 2.0 * COURANT * speed[x] * gathered

    def receivers_at(moment):
        slot = moment if moment < STEPS else 2 * STEPS
        for s in range(shots):
            @pl.loop(0, chunks)
            def _(c):
                block = ext[slot, s, pl.ds(MARGIN + c * chunk, chunk)].reshape(span, width)
                part = jnp.dot(pick[s, c], split_two(block), preferred_element_type=jnp.float32)

                @pl.when(c == 0)
                def _():
                    misfit[...] = part

                @pl.when(c > 0)
                def _():
                    misfit[...] += part

            found = misfit[:, :width] + misfit[:, width:]
            sample = jnp.sum(found * hot[s], axis=1, keepdims=True)
            miss = sample - columns[s, :, moment - 1 : moment]
            values = split_two(miss * hot[s])

            @pl.loop(0, chunks)
            def _(c):
                both = jnp.dot(put[s, c], values, preferred_element_type=jnp.float32)
                landed[moment - 1, s, pl.ds(c * chunk, chunk)] = (
                    both[:, :width] + both[:, width:]
                ).reshape(chunk, depth, width)

    for load in loads[:3]:
        load.wait()
    forward(0, MARGIN, rows - MARGIN)
    receive(0)
    forward(0, 0, MARGIN)
    forward(0, rows - MARGIN, rows)
    send(1)
    receivers_at(1)
    for moment in range(1, STEPS):
        receive(moment)
        forward(moment, 0, MARGIN)
        forward(moment, rows - MARGIN, rows)
        if moment + 1 < STEPS:
            send(moment + 1)
        forward(moment, MARGIN, rows - MARGIN)
        receivers_at(moment + 1)
    for load in loads[3:]:
        load.wait()
    for moment in range(STEPS, 0, -1):
        slot = 2 * STEPS - moment
        receive(slot)
        backward(moment, 0, MARGIN)
        backward(moment, rows - MARGIN, rows)
        if moment > 1:
            send(slot + 1)
        backward(moment, MARGIN, rows - MARGIN)
    for slot in range(2 * STEPS):
        @pl.when(has_left)
        def _():
            copies[slot][0].wait_send()

        @pl.when(has_right)
        def _():
            copies[slot][1].wait_send()


def shot_gradient(
    velocity, prev, now, later, adjoint, wavelet, source_cells, signs, record_cells, observed
):
    shots, rows, depth, width = now.shape
    receivers = record_cells.shape[1]
    chunk = 8
    span = chunk * depth
    hbm = pl.BlockSpec(memory_space=pl.ANY)
    vmem = pl.BlockSpec(memory_space=pltpu.VMEM)
    smem = pl.BlockSpec(memory_space=pltpu.SMEM)
    f32 = jnp.float32
    return pl.pallas_call(
        functools.partial(wave_kernel, lax.axis_size("dom")),
        out_shape=jax.ShapeDtypeStruct((rows, depth, width), f32),
        in_specs=[hbm] * 5 + [smem] * 3 + [vmem] * 2,
        out_specs=vmem,
        scratch_shapes=[
            pltpu.VMEM((2 * STEPS + 1, shots, rows + 2 * MARGIN, depth, width), f32),
            pltpu.VMEM((shots, rows, depth, width), f32),
            pltpu.VMEM((shots, rows, depth, width), f32),
            pltpu.VMEM((rows, depth, width), f32),
            pltpu.VMEM((STEPS, shots, rows, depth, width), f32),
            pltpu.VMEM((shots, rows, depth, width), f32),
            pltpu.VMEM((STEPS, shots, rows, depth, width), f32),
            pltpu.VMEM((shots, rows // chunk, receivers, span), jnp.bfloat16),
            pltpu.VMEM((shots, rows // chunk, span, receivers), jnp.bfloat16),
            pltpu.VMEM((shots, receivers, width), f32),
            pltpu.VMEM((shots, receivers, width), f32),
            pltpu.VMEM((receivers, 2 * width), f32),
            pltpu.VMEM((rows, depth, width), f32),
            pltpu.SemaphoreType.DMA((5,)),
            pltpu.SemaphoreType.DMA((2 * STEPS, 2)),
            pltpu.SemaphoreType.DMA((2 * STEPS, 2)),
        ],
        compiler_params=pltpu.CompilerParams(
            collective_id=0, has_side_effects=True, vmem_limit_bytes=56 * 1024 * 1024
        ),
    )(
        now,
        adjoint,
        prev,
        later,
        velocity,
        wavelet,
        source_cells,
        signs,
        record_cells,
        observed,
    )


def cosine_basis(length):
    wave_index = jnp.arange(length, dtype=jnp.int32)[:, None]
    position = jnp.arange(length, dtype=jnp.int32)[None, :]
    phase = wave_index * (2 * position + 1) % (4 * length)
    angle = math.pi / (2.0 * length) * phase.astype(jnp.float32)
    factor = jnp.where(wave_index == 0, math.sqrt(1.0 / length), math.sqrt(2.0 / length)).astype(
        jnp.float32
    )
    return factor * jnp.cos(angle)


def prior_gain(length, cutoff):
    scaled = jnp.arange(length, dtype=jnp.float32) / float(cutoff)
    return 1.0 / jnp.sqrt(1.0 + scaled)


def precondition(gradient, noise_cols, rate):
    length = gradient.shape[0]
    basis = cosine_basis(length)
    spectrum = prior_gain(length, length // 32)[:, None]
    highest = lax.Precision.HIGHEST
    grad_hat = jnp.dot(basis, gradient.reshape(length, -1), precision=highest)
    noise_hat = jnp.dot(basis, noise_cols.reshape(length, -1), precision=highest)
    weights = spectrum * (-0.5 * rate * spectrum * grad_hat + jnp.sqrt(rate) * noise_hat)
    update = lax.dot_general(basis, weights, (((0,), (0,)), ((), ())), precision=highest)
    return update.reshape(gradient.shape)


def shared_kernel(
    shots,
    doms,
    partial,
    noise,
    basis,
    basis_t,
    gain,
    step_size,
    out,
    folded,
    noise_fold,
    sums,
    own,
    noise_lines,
    grad_lines,
    update,
    returned,
    send_sem,
    recv_sem,
    shot_send,
    shot_recv,
):
    depth, rows, width = shots * folded.shape[1], folded.shape[2], folded.shape[3]
    fold = folded.shape[1]
    lot = fold // doms
    lane_share = width // shots
    me = lax.axis_index("shot")
    here = lax.axis_index("dom")
    dom_peer = [lax.rem(here + o, doms) for o in range(doms)]
    shot_peer = [lax.rem(me + o, shots) for o in range(shots)]

    barrier = pltpu.get_barrier_semaphore()
    for o in range(1, doms):
        pl.semaphore_signal(barrier, inc=1, device_id={"dom": dom_peer[o]}, device_id_type=MESH)
    for o in range(1, shots):
        pl.semaphore_signal(barrier, inc=1, device_id={"shot": shot_peer[o]}, device_id_type=MESH)

    group = lax.broadcasted_iota(jnp.int32, (rows, width), 1) // lane_share

    def fold_lanes(source, target):
        @pl.loop(0, fold)
        def _(level):
            slabs = [
                source[pl.ds(block * fold + level, rows, stride=depth), :]
                for block in range(shots)
            ]
            for share in range(shots):
                merged = None
                for block in range(shots):
                    shift = (block - share) * lane_share % width
                    turned = pltpu.roll(slabs[block], shift, 1) if shift else slabs[block]
                    merged = turned if merged is None else jnp.where(group == block, turned, merged)
                target[share, level] = merged

    def exchange(phase, source_of, target):
        moves = []
        for o in range(1, doms):
            moves.append(
                pltpu.make_async_remote_copy(
                    src_ref=source_of(dom_peer[o]),
                    dst_ref=target.at[here],
                    send_sem=send_sem.at[phase, o],
                    recv_sem=recv_sem.at[phase, o],
                    device_id={"dom": dom_peer[o]},
                    device_id_type=MESH,
                )
            )
        return moves

    fold_lanes(partial, folded)
    pl.semaphore_wait(barrier, doms + shots - 2)
    sharing = []
    for o in range(1, shots):
        move = pltpu.make_async_remote_copy(
            src_ref=folded.at[shot_peer[o]],
            dst_ref=sums.at[o],
            send_sem=shot_send.at[o],
            recv_sem=shot_recv.at[o],
            device_id={"shot": shot_peer[o]},
            device_id_type=MESH,
        )
        move.start()
        sharing.append(move)
    fold_lanes(noise, noise_fold)
    noise_moves = exchange(0, lambda d: noise_fold.at[me, pl.ds(d * lot, lot)], noise_lines)
    for move in noise_moves:
        move.start()
    noise_lines[here] = noise_fold[me, pl.ds(here * lot, lot)]
    for move in noise_moves:
        move.wait_recv()
    rate = step_size[0]
    highest = lax.Precision.HIGHEST
    lines = doms * rows
    noise_hats = [
        jnp.dot(
            basis[...],
            noise_lines[:, i].reshape(lines, width),
            precision=highest,
            preferred_element_type=jnp.float32,
        )
        for i in range(lot)
    ]
    root = jnp.sqrt(jnp.full((1, 1), rate, jnp.float32))
    for move in sharing:
        move.wait_recv()
    gathered = folded[me]
    for o in range(1, shots):
        gathered = gathered + sums[o]
    own[...] = gathered
    grad_moves = exchange(1, lambda d: own.at[pl.ds(d * lot, lot)], grad_lines)
    for move in grad_moves:
        move.start()
    grad_lines[here] = own[pl.ds(here * lot, lot)]
    for move in grad_moves:
        move.wait_recv()
    for i in range(lot):
        grad_hat = jnp.dot(
            basis[...],
            grad_lines[:, i].reshape(lines, width),
            precision=highest,
            preferred_element_type=jnp.float32,
        )
        weights = gain[...] * (-0.5 * rate * gain[...] * grad_hat + root * noise_hats[i])
        update[:, i] = jnp.dot(
            basis_t[...], weights, precision=highest, preferred_element_type=jnp.float32
        ).reshape(doms, rows, width)
    back_moves = exchange(2, lambda d: update.at[d], returned)
    for move in back_moves:
        move.start()
    returned[here] = update[here]
    for move in back_moves:
        move.wait_recv()
    for d in range(doms):
        for i in range(lot):
            line = returned[d, i]
            for block in range(shots):
                shift = -block * lane_share % width
                turned = pltpu.roll(line, shift, 1) if shift else line
                out[pl.ds(block * fold + d * lot + i, rows, stride=depth), :] = turned
    for move in sharing + noise_moves + grad_moves + back_moves:
        move.wait_send()


def shared_update(partial_value, noise_field, step_size):
    rows, depth, width = partial_value.shape
    shots, doms = lax.axis_size("shot"), lax.axis_size("dom")
    length = rows * doms
    fold = depth // shots
    lot = fold // doms
    wave = np.arange(length)[:, None]
    phase = wave * (2 * np.arange(length)[None, :] + 1) % (4 * length)
    factor = np.where(wave == 0, math.sqrt(1.0 / length), math.sqrt(2.0 / length))
    basis = (factor * np.cos(math.pi / (2.0 * length) * phase)).astype(np.float32)
    gain = (1.0 / np.sqrt(1.0 + wave / (length // 32))).astype(np.float32)
    f32 = jnp.float32
    vmem = pl.BlockSpec(memory_space=pltpu.VMEM)
    smem = pl.BlockSpec(memory_space=pltpu.SMEM)
    result = pl.pallas_call(
        functools.partial(shared_kernel, shots, doms),
        out_shape=jax.ShapeDtypeStruct((rows * depth, width), f32),
        in_specs=[vmem] * 5 + [smem],
        out_specs=vmem,
        scratch_shapes=[
            pltpu.VMEM((shots, fold, rows, width), f32),
            pltpu.VMEM((shots, fold, rows, width), f32),
            pltpu.VMEM((shots, fold, rows, width), f32),
            pltpu.VMEM((fold, rows, width), f32),
            pltpu.VMEM((doms, lot, rows, width), f32),
            pltpu.VMEM((doms, lot, rows, width), f32),
            pltpu.VMEM((doms, lot, rows, width), f32),
            pltpu.VMEM((doms, lot, rows, width), f32),
            pltpu.SemaphoreType.DMA((3, doms)),
            pltpu.SemaphoreType.DMA((3, doms)),
            pltpu.SemaphoreType.DMA((shots,)),
            pltpu.SemaphoreType.DMA((shots,)),
        ],
        compiler_params=pltpu.CompilerParams(
            collective_id=1, has_side_effects=True, vmem_limit_bytes=32 * 1024 * 1024
        ),
    )(
        partial_value.reshape(rows * depth, width),
        noise_field.reshape(rows * depth, width),
        jnp.asarray(basis),
        jnp.asarray(np.ascontiguousarray(basis.T)),
        jnp.asarray(gain),
        step_size,
    )
    return result.reshape(rows, depth, width)[:, :, : width // shots]


def body(
    velocity,
    noise_field,
    step_size,
    field_prev,
    field_now,
    adjoint_next,
    adjoint_now,
    wavelet,
    source_cells,
    source_signs,
    record_cells,
    observed,
):
    partial_value = shot_gradient(
        velocity,
        field_prev,
        field_now,
        adjoint_next,
        adjoint_now,
        wavelet,
        source_cells,
        source_signs,
        record_cells,
        observed,
    )
    rate = step_size[0]
    shot_rows = velocity.shape[2] // lax.axis_size("shot")
    start = lax.axis_index("shot") * shot_rows
    if velocity.shape[1] % (lax.axis_size("shot") * lax.axis_size("dom")) == 0:
        moved = shared_update(partial_value, noise_field, step_size)
        return lax.dynamic_slice_in_dim(velocity, start, shot_rows, 2) + moved
    share = lax.psum_scatter(partial_value, "shot", scatter_dimension=2, tiled=True)
    noise_part = lax.dynamic_slice_in_dim(noise_field, start, shot_rows, 2)
    grad_cols, noise_cols = (
        lax.all_to_all(share, "dom", split_axis=2, concat_axis=0, tiled=True),
        lax.all_to_all(noise_part, "dom", split_axis=2, concat_axis=0, tiled=True),
    )
    update = precondition(grad_cols, noise_cols, rate)
    returned = lax.all_to_all(update, "dom", split_axis=0, concat_axis=2, tiled=True)
    result = lax.dynamic_slice_in_dim(velocity, start, shot_rows, 2) + returned
    return result


def solution(mesh):
    placed = (
        P("dom", None, None),
        P("dom", None, None),
        P(),
        P("shot", "dom", None, None),
        P("shot", "dom", None, None),
        P("shot", "dom", None, None),
        P("shot", "dom", None, None),
        P("shot", None),
        P("shot", None),
        P("shot", None),
        P("shot", None),
        P("shot", None, None),
    )
    return jax.shard_map(
        body, mesh=mesh, in_specs=placed, out_specs=P("dom", None, "shot"), check_vma=False
    )
```

profile of v0, /device:TPU:0, one launch (start us, length us, event | category | flops | bytes accessed | tf_op | source)
XLA Modules:
  0.0 71.4 jit_solution(596443862660503919)
XLA Ops:
  0.0 0.0 copy-start.2
  0.0 0.0 copy-start.3
  0.0 0.0 copy-start.4
  0.0 0.0 copy-start.1
  0.0 44.7 %shard_map.145 = f32[32,32,128]{2,1,0:T(8,128)} custom-call(f32[2,32,32,128]{3,2,1,0:T(8,128)} %now_hbm.1, f32[2,32,32,128]{3,2,1,0:T(8,128)} %adj_hbm.1, f32[2,32,32,128]{3,2,1,0:T(8,128)} %prev_hbm.1, f32[2,32,32,128]{3,2,1,0:T(8,128)} %later_hbm.1, f32[32,32,128]{2,1,0:T(8,128)} %speed_hbm.1, f32[2,4]{1,0:T(2,128)} %pulse.1, s32[2,8]{1,0:T(2,128)} %src_cells.1, ...), custom_call_target="tpu_custom_call" | custom-call | tf_op jit(solution)/shard_map/pallas_call | solution.py:320
  45.3 0.0 copy-done.2
  45.3 0.0 copy-done.3
  45.3 0.0 copy-done.4
  45.4 0.0 copy-done.1
  45.4 0.0 copy-start
  45.4 1.0 %copy-done = f32[32,32,128]{2,1,0:T(8,128)S(1)} copy-done((f32[32,32,128]{2,1,0:T(8,128)S(1)}, f32[32,32,128]{2,1,0:T(8,128)}, u32[]{:S(2)}) %copy-start) | copy-done | bytes 524312
  46.4 0.0 copy-start.5
  46.4 24.0 %shard_map.146 = f32[1024,128]{1,0:T(8,128)S(1)} custom-call(f32[1024,128]{1,0:T(8,128)S(1)} %bitcast.3, f32[1024,128]{1,0:T(8,128)S(1)} %bitcast.5, f32[256,256]{1,0:T(8,128)S(1)} %copy-done.2, f32[256,256]{1,0:T(8,128)S(1)} %copy-done.3, f32[256,1]{1,0:T(8,128)S(1)} %copy-done.4, f32[1]{0:T(128)S(6)} %copy.16.step_size), custom_call_target="tpu_custom_call" | custom-call | tf_op jit(solution)/shard_map/pallas_call | solution.py:546
  70.4 0.0 copy-done.5
  70.4 1.0 %slice_add_fusion = f32[32,32,32]{2,1,0:T(8,128)} fusion(f32[32,32,128]{2,1,0:T(8,128)S(1)} %bitcast.4, f32[32,32,128]{2,1,0:T(8,128)S(1)} %copy-done.5, s32[]{:T(128)S(6)} %select_n.3), kind=kLoop, calls=%fused_computation | loop fusion | flops 32768 | bytes 393220 | tf_op jit(solution)/shard_map/add | solution.py:610
Async XLA Ops:
  0.0 45.3 %copy-start.2 = (f32[256,256]{1,0:T(8,128)S(1)}, f32[256,256]{1,0:T(8,128)}, u32[]{:S(2)}) copy-start(f32[256,256]{1,0:T(8,128)} %constant.17.clone.basis) | copy-start | bytes 786436
  0.0 45.3 %copy-start.3 = (f32[256,256]{1,0:T(8,128)S(1)}, f32[256,256]{1,0:T(8,128)}, u32[]{:S(2)}) copy-start(f32[256,256]{1,0:T(8,128)} %constant.18.clone.basis_t) | copy-start | bytes 786436
  0.0 45.3 %copy-start.4 = (f32[256,1]{1,0:T(8,128)S(1)}, f32[256,1]{1,0:T(8,128)}, u32[]{:S(2)}) copy-start(f32[256,1]{1,0:T(8,128)} %constant.19.clone.gain) | copy-start | bytes 3076
  0.0 45.3 %copy-start.1 = (f32[32,32,128]{2,1,0:T(8,128)S(1)}, f32[32,32,128]{2,1,0:T(8,128)}, u32[]{:S(2)}) copy-start(f32[32,32,128]{2,1,0:T(8,128)} %param.16) | copy-start | bytes 1572868
  45.4 1.0 %copy-start = (f32[32,32,128]{2,1,0:T(8,128)S(1)}, f32[32,32,128]{2,1,0:T(8,128)}, u32[]{:S(2)}) copy-start(f32[32,32,128]{2,1,0:T(8,128)} %shard_map.145) | copy-start | bytes 1572868
  46.4 24.0 %copy-start.5 = (f32[32,32,128]{2,1,0:T(8,128)S(1)}, f32[32,32,128]{2,1,0:T(8,128)}, u32[]{:S(2)}) copy-start(f32[32,32,128]{2,1,0:T(8,128)} %speed_hbm.1) | copy-start | bytes 1572868
where the time goes:
time: 71.6 us; the launch traced here: 71.4 us
  Pallas kernels  68.6 us (96%)
  local copies, waits for them, and re-layouts  1.05 us (1%)
  other arithmetic  1 us (1%)
  between operations  0.72 us (1%)
    pallas_call x1, Pallas kernels, shot_gradient(): pl.pallas_call(functools.partial(wave_kernel, lax.axis_size('dom')), out_...  44.7 us
    pallas_call x1, Pallas kernels, shared_update(): pl.pallas_call(functools.partial(shared_kernel, shots, doms), out_shape=j...  24 us

commit v1 on v0

--- a/solution.py
+++ b/solution.py
@@ -20,10 +20,28 @@
 MESH = pl.DeviceIdType.MESH
 
 
+REACH = 2 * MARGIN
+BORDER = 3 * MARGIN
+WEIGHTS = (-43050.0, 8064.0, -1008.0, 128.0, -9.0)
+SCALE = 5040.0
+
+
 def split_two(value):
     high = value.astype(jnp.bfloat16)
     low = (value - high.astype(jnp.float32)).astype(jnp.bfloat16)
-    return jnp.concatenate([high, low], axis=-1)
+    return high, low
+
+
+def banded(size, block, centre):
+    down = lax.broadcasted_iota(jnp.int32, (size, size), 0)
+    over = lax.broadcasted_iota(jnp.int32, (size, size), 1)
+    apart = jnp.abs(down - over)
+    band = jnp.where(apart == 0, centre, 0.0)
+    for r in range(1, MARGIN + 1):
+        band = jnp.where(apart == r, WEIGHTS[r], band)
+    if block < size:
+        band = jnp.where(down // block == over // block, band, 0.0)
+    return band.astype(jnp.bfloat16)
 
 
 def wave_kernel(
@@ -39,38 +57,63 @@
     record_cells,
     observed,
     out,
-    ext,
+    f0,
+    f1,
+    f2,
+    f3,
+    f4,
+    a4,
+    a3,
+    a2,
+    a1,
     prev,
     later,
     speed,
+    squares,
     laps,
+    mf0,
+    mf1,
+    ma0,
+    ma1,
+    hf0,
+    hf1,
+    ha,
+    across_y,
+    across_z,
     spread_src,
     landed,
     pick,
     put,
     hot,
     columns,
-    misfit,
+    measured,
+    found,
+    beside,
+    values,
     total,
     load_sem,
     send_sem,
     recv_sem,
 ):
+    fields = (f0, f1, f2, f3, f4)
+    mf, hf, ma = (mf0, mf1), (hf0, hf1), (ma0, ma1)
     shots, rows, depth, width = prev.shape
     here = lax.axis_index("dom")
     left = jnp.maximum(here - 1, 0)
     right = jnp.minimum(here + 1, doms - 1)
     has_left = here > 0
     has_right = here < doms - 1
-    chunk = 8
-    chunks = rows // chunk
-    high_start = rows + MARGIN
+    group = MARGIN
+    groups = rows // group
+    half = 16
+    halves = depth // half
+    f32 = jnp.float32
 
     loads = [
-        pltpu.make_async_copy(now_hbm, ext.at[0, :, pl.ds(MARGIN, rows)], load_sem.at[0]),
-        pltpu.make_async_copy(speed_hbm, speed, load_sem.at[1]),
+        pltpu.make_async_copy(now_hbm, f0.at[:, pl.ds(MARGIN, rows)], load_sem.at[0]),
+        pltpu.make_async_copy(speed_hbm, speed.at[pl.ds(REACH, rows)], load_sem.at[1]),
         pltpu.make_async_copy(prev_hbm, prev, load_sem.at[2]),
-        pltpu.make_async_copy(adj_hbm, ext.at[STEPS, :, pl.ds(MARGIN, rows)], load_sem.at[3]),
+        pltpu.make_async_copy(adj_hbm, a4.at[:, pl.ds(BORDER, rows)], load_sem.at[3]),
         pltpu.make_async_copy(later_hbm, later, load_sem.at[4]),
     ]
     for load in loads:
@@ -88,222 +131,453 @@
 
     pl.semaphore_wait(barrier, has_left.astype(jnp.int32) + has_right.astype(jnp.int32))
 
-    def halo_copies(slot, source):
-        base = MARGIN if source is None else 0
-        field = ext.at[slot] if source is None else source
+    pairs = []
+
+    def pair(low_source, high_target, high_source, low_target):
+        index = len(pairs)
         to_left = pltpu.make_async_remote_copy(
-            src_ref=field.at[:, pl.ds(base, MARGIN)],
-            dst_ref=ext.at[slot, :, pl.ds(high_start, MARGIN)],
-            send_sem=send_sem.at[slot, 0],
-            recv_sem=recv_sem.at[slot, 1],
+            src_ref=low_source,
+            dst_ref=high_target,
+            send_sem=send_sem.at[index, 0],
+            recv_sem=recv_sem.at[index, 1],
             device_id={"dom": left},
             device_id_type=MESH,
         )
         to_right = pltpu.make_async_remote_copy(
-            src_ref=field.at[:, pl.ds(base + rows - MARGIN, MARGIN)],
-            dst_ref=ext.at[slot, :, pl.ds(0, MARGIN)],
-            send_sem=send_sem.at[slot, 1],
-            recv_sem=recv_sem.at[slot, 0],
+            src_ref=high_source,
+            dst_ref=low_target,
+            send_sem=send_sem.at[index, 1],
+            recv_sem=recv_sem.at[index, 0],
             device_id={"dom": right},
             device_id_type=MESH,
         )
-        return to_left, to_right
-
-    copies = [
-        halo_copies(slot, {0: now_hbm, STEPS: adj_hbm}.get(slot)) for slot in range(2 * STEPS)
-    ]
-
-    def send(slot):
+        pairs.append((to_left, to_right))
+        return pairs[-1]
+
+    def send(copies):
         @pl.when(has_left)
         def _():
-            copies[slot][0].start()
+            copies[0].start()
 
         @pl.when(has_right)
         def _():
-            copies[slot][1].start()
-
-    def receive(slot):
+            copies[1].start()
+
+    def receive(copies):
         @pl.when(has_left)
         def _():
-            copies[slot][1].wait_recv()
+            copies[1].wait_recv()
 
         @pl.when(has_right)
         def _():
-            copies[slot][0].wait_recv()
-
-    send(0)
-    send(STEPS)
-
-    edge = jnp.zeros((2 * STEPS, shots, MARGIN, depth, width), jnp.float32)
+            copies[0].wait_recv()
+
+    def sent(copies):
+        @pl.when(has_left)
+        def _():
+            copies[0].wait_send()
+
+        @pl.when(has_right)
+        def _():
+            copies[1].wait_send()
+
+    halos = []
+    for k in range(STEPS):
+        halos.append([])
+        for s in range(shots):
+            field = fields[k]
+            source = now_hbm if k == 0 else field
+            base = 0 if k == 0 else MARGIN
+            halos[k].append(
+                pair(
+                    source.at[s, pl.ds(base, MARGIN)],
+                    field.at[s, pl.ds(MARGIN + rows, MARGIN)],
+                    source.at[s, pl.ds(base + rows - MARGIN, MARGIN)],
+                    field.at[s, pl.ds(0, MARGIN)],
+                )
+            )
+    adj_halo = pair(
+        adj_hbm.at[:, pl.ds(0, REACH)],
+        a4.at[:, pl.ds(BORDER + rows, REACH)],
+        adj_hbm.at[:, pl.ds(rows - REACH, REACH)],
+        a4.at[:, pl.ds(BORDER - REACH, REACH)],
+    )
+    speed_halo = pair(
+        speed_hbm.at[pl.ds(0, REACH)],
+        speed.at[pl.ds(REACH + rows, REACH)],
+        speed_hbm.at[pl.ds(rows - REACH, REACH)],
+        speed.at[pl.ds(0, REACH)],
+    )
+    border_halo = pair(
+        a3.at[:, pl.ds(BORDER, BORDER)],
+        a3.at[:, pl.ds(BORDER + rows, BORDER)],
+        a3.at[:, pl.ds(rows, BORDER)],
+        a3.at[:, pl.ds(0, BORDER)],
+    )
+    samples = [
+        pair(found.at[k], beside.at[k, 1], found.at[k], beside.at[k, 0]) for k in range(STEPS)
+    ]
+
+    for s in range(shots):
+        send(halos[0][s])
+    send(adj_halo)
+    send(speed_halo)
+
+    def clear(first_field, first_adj, first_border, first_speed, side):
+        for k in range(STEPS):
+            for s in range(shots):
+                fields[k][s, pl.ds(first_field, MARGIN)] = jnp.zeros((MARGIN, depth, width), f32)
+        for s in range(shots):
+            a4[s, pl.ds(first_adj, REACH)] = jnp.zeros((REACH, depth, width), f32)
+            a3[s, pl.ds(first_border, BORDER)] = jnp.zeros((BORDER, depth, width), f32)
+        speed[pl.ds(first_speed, REACH)] = jnp.zeros((REACH, depth, width), f32)
+        for k in range(STEPS):
+            beside[k, side] = jnp.zeros(beside.shape[2:], f32)
 
     @pl.when(jnp.logical_not(has_left))
     def _():
-        ext[pl.ds(0, 2 * STEPS), :, pl.ds(0, MARGIN)] = edge
+        clear(0, BORDER - REACH, 0, 0, 0)
 
     @pl.when(jnp.logical_not(has_right))
     def _():
-        ext[pl.ds(0, 2 * STEPS), :, pl.ds(high_start, MARGIN)] = edge
-
-    lanes = lax.broadcasted_iota(jnp.int32, (depth, width), 1)
-    nothing = jnp.zeros((MARGIN, width), jnp.float32)
-
-    span = chunk * depth
+        clear(MARGIN + rows, BORDER + rows, BORDER + rows, REACH + rows, 1)
+
+    across_y[...] = jnp.concatenate([banded(width, width, -43008.0)] * 2, axis=0)
+    across_z[...] = jnp.concatenate([banded(group * depth, depth, -42.0)] * 2, axis=1)
+
     receivers = record_cells.shape[1]
+    tiles = receivers // 8
+    lane = lax.broadcasted_iota(jnp.int32, (8, width), 1)
     first = here * (rows * depth)
     row_of = lambda cell: lax.div(cell, jnp.int32(width))
     lane_of = lambda cell: lax.rem(cell, jnp.int32(width))
     tile = (width, receivers)
     place = lax.broadcasted_iota(jnp.int32, tile, 0)
+    span = 8 * depth
+    compact = [jnp.zeros((8, width), f32) for _ in range(STEPS)]
     for s in range(shots):
         cells = record_cells[s : s + 1, :]
         rec_rows = row_of(cells) - first
         table = jnp.where(
             place == STEPS,
-            jnp.broadcast_to(rec_rows.astype(jnp.float32), tile),
-            jnp.broadcast_to(lane_of(cells).astype(jnp.float32), tile),
+            jnp.broadcast_to(rec_rows.astype(f32), tile),
+            jnp.broadcast_to(lane_of(cells).astype(f32), tile),
         )
         for k in range(STEPS):
             table = jnp.where(place == k, jnp.broadcast_to(observed[s, k : k + 1, :], tile), table)
         columns[s] = jnp.transpose(table)
         rec_col = columns[s, :, STEPS : STEPS + 1].astype(jnp.int32)
         rec_lane = columns[s, :, STEPS + 1 : STEPS + 2].astype(jnp.int32)
-        hot[s] = (lax.broadcasted_iota(jnp.int32, (receivers, width), 1) == rec_lane).astype(
-            jnp.float32
-        )
+        hot[s] = (lax.broadcasted_iota(jnp.int32, (receivers, width), 1) == rec_lane).astype(f32)
+        for k in range(STEPS):
+            for j in range(tiles):
+                column = columns[s, pl.ds(j * 8, 8), k : k + 1]
+                compact[k] = jnp.where(lane == s * tiles + j, column, compact[k])
         count = src_cells.shape[1]
         padded = count + (-count) % 128
         order = lax.broadcasted_iota(jnp.int32, (padded, width), 0)
         across = lax.broadcasted_iota(jnp.int32, (padded, width), 1)
         along = lax.broadcasted_iota(jnp.int32, (1, padded), 1)
-        tall = jnp.zeros((padded, width), jnp.float32)
+        tall = jnp.zeros((padded, width), f32)
         src_rows = jnp.full((1, padded), -1, jnp.int32)
         for j in range(count):
             cell = src_cells[s, j]
-            sign = (2 * src_signs[s, j] - 1).astype(jnp.float32)
+            sign = (2 * src_signs[s, j] - 1).astype(f32)
             tall = jnp.where((order == j) & (across == lane_of(cell)), sign, tall)
             src_rows = jnp.where(along == j, row_of(cell) - first, src_rows)
         tall = tall.astype(jnp.bfloat16)
 
-        @pl.loop(0, chunks)
+        for c in range(rows * depth // span):
+            cell = lax.broadcasted_iota(jnp.int32, (receivers, span), 1) + c * span
+            pick[s, :, c * span : (c + 1) * span] = (
+                (cell == rec_col).astype(f32).astype(jnp.bfloat16)
+            )
+
+        @pl.loop(0, rows * depth // span)
         def _(c):
-            cell = lax.broadcasted_iota(jnp.int32, (receivers, span), 1) + c * span
-            pick[s, c] = (cell == rec_col).astype(jnp.float32).astype(jnp.bfloat16)
-            cell = lax.broadcasted_iota(jnp.int32, (span, receivers), 0) + c * span
-            put[s, c] = (cell == rec_rows).astype(jnp.float32).astype(jnp.bfloat16)
             cell = lax.broadcasted_iota(jnp.int32, (span, padded), 0) + c * span
-            wide = (cell == src_rows).astype(jnp.float32).astype(jnp.bfloat16)
-            spots = jnp.dot(wide, tall, preferred_element_type=jnp.float32)
-            spread_src[s, pl.ds(c * chunk, chunk)] = spots.reshape(chunk, depth, width)
-
-    def laplacian(slot, s, x):
-        middle = ext[slot, s, x + MARGIN]
-        summed = 3.0 * COEFFS[0] * middle
-        for r in range(1, MARGIN + 1):
-            beside = ext[slot, s, x + MARGIN + r] + ext[slot, s, x + MARGIN - r]
-            beside += jnp.concatenate([middle[r:], nothing[:r]], axis=0)
-            beside += jnp.concatenate([nothing[:r], middle[: depth - r]], axis=0)
-            beside += jnp.where(lanes < width - r, pltpu.roll(middle, width - r, 1), 0.0)
-            beside += jnp.where(lanes >= r, pltpu.roll(middle, r, 1), 0.0)
-            summed += COEFFS[r] * beside
-        return middle, summed
-
-    def forward(moment, first, last):
-        @pl.loop(first, last, unroll=MARGIN)
+            wide = (cell == src_rows).astype(f32).astype(jnp.bfloat16)
+            spots = jnp.dot(wide, tall, preferred_element_type=f32)
+            spread_src[s, pl.ds(c * 8, 8)] = spots.reshape(8, depth, width)
+
+        @pl.loop(0, (rows + 2 * BORDER) // 8)
+        def _(c):
+            cell = lax.broadcasted_iota(jnp.int32, (span, receivers), 0)
+            cell = cell + (c * span - BORDER * depth)
+            put[s, pl.ds(pl.multiple_of(c * span, span), span)] = (
+                (cell == rec_rows).astype(f32).astype(jnp.bfloat16)
+            )
+
+    for k in range(STEPS):
+        measured[k] = compact[k]
+
+    def keep_split(ref, s, row, part, value):
+        high, low = split_two(value)
+        ref[s, row, part, 0:width] = high
+        ref[s, row, part, width : 2 * width] = low
+
+    def product(split, split_row, target, target_row):
+        lines = [
+            split[s, pl.ds(split_row, group)].reshape(group * depth, 2 * width)
+            for s in range(shots)
+        ]
+        highs = jnp.concatenate([line[:, :width] for line in lines], axis=1)
+        lows = jnp.concatenate([line[:, width:] for line in lines], axis=1)
+        down = jnp.dot(
+            across_z[...], jnp.concatenate([highs, lows], axis=0), preferred_element_type=f32
+        )
+        for s in range(shots):
+            over = jnp.dot(lines[s], across_y[...], preferred_element_type=f32)
+            both = over + down[:, s * width : (s + 1) * width]
+            target[s, pl.ds(target_row, group)] = both.reshape(group, depth, width)
+
+    def beside_x(window, i):
+        summed = WEIGHTS[1] * (window[i + 3] + window[i + 5])
+        for r in range(2, MARGIN + 1):
+            summed += WEIGHTS[r] * (window[i + MARGIN + r] + window[i + MARGIN - r])
+        return summed
+
+    def sweep(first, last, point, product_of):
+        point(first)
+
+        @pl.loop(first + 1, last)
+        def _(g):
+            product_of(g - 1)
+            point(g)
+
+        product_of(last - 1)
+
+    def square(first, last):
+        @pl.loop(first, last)
         def _(x):
-            squared = COURANT * speed[x] * speed[x]
+            squares[x] = (COURANT / SCALE) * speed[x] * speed[x]
+
+    parts = [pl.ds(h * half, half) for h in range(halves)]
+
+    def prepare(field, margin, split, split_margin, target, target_margin):
+        def point(g):
             for s in range(shots):
-                middle, summed = laplacian(moment, s, x)
-                before = prev[s, x] if moment == 0 else ext[moment - 1, s, x + MARGIN]
-                laps[moment, s, x] = summed
-                slot = moment + 1 if moment + 1 < STEPS else 2 * STEPS
-                ext[slot, s, x + MARGIN] = (
-                    2.0 * middle - before + squared * summed + pulse[s, moment] * spread_src[s, x]
+                for i in range(group):
+                    for part in parts:
+                        x = g * group + i
+                        keep_split(split, s, x + split_margin, part, field[s, x + margin, part])
+
+        sweep(
+            0,
+            groups,
+            point,
+            lambda g: product(split, g * group + split_margin, target, g * group + target_margin),
+        )
+
+    def forward_point(k, g, which):
+        x = g * group
+        field, target, split = fields[k], fields[k + 1], hf[(k + 1) % 2]
+        for part in parts:
+            for s in which:
+                window = [field[s, x + i, part] for i in range(group + 2 * MARGIN)]
+                for i in range(group):
+                    lap = mf[k % 2][s, x + i, part] + beside_x(window, i)
+                    laps[k, s, x + i, part] = lap
+                    if k == 0:
+                        before = prev[s, x + i, part]
+                    else:
+                        before = fields[k - 1][s, x + i + MARGIN, part]
+                    fresh = 2.0 * window[i + MARGIN] - before
+                    fresh = fresh + pulse[s, k] * spread_src[s, x + i, part]
+                    fresh = fresh + squares[x + i + REACH, part] * lap
+                    target[s, x + i + MARGIN, part] = fresh
+                    keep_split(split, s, x + i, part, fresh)
+
+    def forward_product(k, g):
+        product(hf[(k + 1) % 2], g * group, mf[(k + 1) % 2], g * group)
+
+    def forward_inside(k):
+        sweep(
+            1,
+            groups - 1,
+            lambda g: forward_point(k, g, range(shots)),
+            lambda g: forward_product(k, g) if k + 1 < STEPS else None,
+        )
+
+    def sample(k):
+        split = hf[(k + 1) % 2]
+        gathered = jnp.zeros((8, width), f32)
+        for s in range(shots):
+            both = jnp.dot(
+                pick[s],
+                split[s].reshape(rows * depth, 2 * width),
+                preferred_element_type=f32,
+            )
+            chosen = (both[:, :width] + both[:, width:]) * hot[s]
+            column = jnp.sum(chosen, axis=1, keepdims=True)
+            for j in range(tiles):
+                gathered = jnp.where(
+                    lane == s * tiles + j, column[j * 8 : (j + 1) * 8], gathered
                 )
-
-    def backward(moment, first, last):
-        slot = 2 * STEPS - moment
-
-        @pl.loop(first, last, unroll=MARGIN)
-        def _(x):
-            squared = COURANT * speed[x] * speed[x]
-            gathered = None
+        found[k] = gathered
+
+    def misfits(k, everywhere):
+        missed = found[k] - measured[k]
+        if everywhere:
+            missed = missed + (beside[k, 0] + beside[k, 1])
+        for s in range(shots):
+            for j in range(0, tiles, 2):
+                block = []
+                for t in (j, j + 1):
+                    at = s * tiles + t
+                    block.append(missed[:, at : at + 1] * hot[s, pl.ds(t * 8, 8)])
+                high, low = split_two(jnp.concatenate(block, axis=0))
+                values[s, pl.ds(j * 8, 16), 0:width] = high
+                values[s, pl.ds(j * 8, 16), width : 2 * width] = low
+
+    def dropped(s, x, count):
+        at = pl.multiple_of((x + BORDER) * depth, group * depth)
+        both = jnp.dot(put[s, pl.ds(at, count * depth)], values[s], preferred_element_type=f32)
+        return (both[:, :width] + both[:, width:]).reshape(count, depth, width)
+
+    def land(k, extra):
+        @pl.loop(-extra // 8, (rows + extra) // 8)
+        def _(c):
             for s in range(shots):
-                middle, summed = laplacian(slot, s, x)
-                after = later[s, x] if moment == STEPS else ext[slot - 1, s, x + MARGIN]
-                earlier = 2.0 * middle - after + squared * summed + landed[moment - 1, s, x]
-                if moment > 1:
-                    ext[slot + 1, s, x + MARGIN] = earlier
-                term = earlier * laps[moment - 1, s, x]
+                landed[k, s, pl.ds(c * 8 + REACH, 8)] = dropped(s, c * 8, 8)
+
+    def free_point(g):
+        x = g * group
+        for part in parts:
+            for s in range(shots):
+                window = [
+                    a4[s, x + BORDER - MARGIN + i, part] for i in range(group + 2 * MARGIN)
+                ]
+                for i in range(group):
+                    lap = ma0[s, x + i + BORDER, part] + beside_x(window, i)
+                    fresh = 2.0 * window[i + MARGIN] - later[s, x + i, part]
+                    a3[s, x + i + BORDER, part] = fresh + squares[x + i + REACH, part] * lap
+
+    def drop_point(g, inside):
+        x = g * group
+        gathered = None
+        for s in range(shots):
+            fresh = a3[s, pl.ds(x + BORDER, group)] + dropped(s, x, group)
+            a3[s, pl.ds(x + BORDER, group)] = fresh
+            high, low = split_two(fresh)
+            ha[s, pl.ds(x + BORDER, group), :, 0:width] = high
+            ha[s, pl.ds(x + BORDER, group), :, width : 2 * width] = low
+            if inside:
+                term = fresh * laps[STEPS - 1, s, pl.ds(x, group)]
                 gathered = term if gathered is None else gathered + term
-            if moment < STEPS:
-                gathered = gathered + total[x]
-            if moment > 1:
-                total[x] = gathered
-            else:
-                out[x] = 2.0 * COURANT * speed[x] * gathered
-
-    def receivers_at(moment):
-        slot = moment if moment < STEPS else 2 * STEPS
-        for s in range(shots):
-            @pl.loop(0, chunks)
-            def _(c):
-                block = ext[slot, s, pl.ds(MARGIN + c * chunk, chunk)].reshape(span, width)
-                part = jnp.dot(pick[s, c], split_two(block), preferred_element_type=jnp.float32)
-
-                @pl.when(c == 0)
-                def _():
-                    misfit[...] = part
-
-                @pl.when(c > 0)
-                def _():
-                    misfit[...] += part
-
-            found = misfit[:, :width] + misfit[:, width:]
-            sample = jnp.sum(found * hot[s], axis=1, keepdims=True)
-            miss = sample - columns[s, :, moment - 1 : moment]
-            values = split_two(miss * hot[s])
-
-            @pl.loop(0, chunks)
-            def _(c):
-                both = jnp.dot(put[s, c], values, preferred_element_type=jnp.float32)
-                landed[moment - 1, s, pl.ds(c * chunk, chunk)] = (
-                    both[:, :width] + both[:, width:]
-                ).reshape(chunk, depth, width)
+        if inside:
+            total[pl.ds(x, group)] = gathered
+
+    adj = {4: a4, 3: a3, 2: a2, 1: a1}
+    adj_mix = {4: ma0, 3: ma1, 2: ma0, 1: ma1}
+
+    def adj_product(m, g):
+        product(ha, g * group + BORDER, adj_mix[m], g * group + BORDER)
+
+    def backward_point(m, g, inside):
+        x = g * group
+        field, after = adj[m], adj[m + 1]
+        for part in parts:
+            gathered = [None] * group
+            for s in range(shots):
+                window = [
+                    field[s, x + BORDER - MARGIN + i, part] for i in range(group + 2 * MARGIN)
+                ]
+                for i in range(group):
+                    lap = adj_mix[m][s, x + i + BORDER, part] + beside_x(window, i)
+                    fresh = 2.0 * window[i + MARGIN] - after[s, x + i + BORDER, part]
+                    fresh = fresh + landed[m - 1, s, x + i + REACH, part]
+                    fresh = fresh + squares[x + i + REACH, part] * lap
+                    if m > 1:
+                        adj[m - 1][s, x + i + BORDER, part] = fresh
+                        keep_split(ha, s, x + i + BORDER, part, fresh)
+                    if inside:
+                        term = fresh * laps[m - 1, s, x + i, part]
+                        gathered[i] = term if gathered[i] is None else gathered[i] + term
+            if inside:
+                for i in range(group):
+                    summed = total[x + i, part] + gathered[i]
+                    if m > 1:
+                        total[x + i, part] = summed
+                    else:
+                        factor = (2.0 * COURANT / SCALE) * speed[x + i + REACH, part]
+                        out[x + i, part] = factor * summed
+
+    def backward(m, first, last, inside):
+        sweep(
+            first,
+            last,
+            lambda g: backward_point(m, g, inside),
+            lambda g: adj_product(m - 1, g) if m > 1 else None,
+        )
 
     for load in loads[:3]:
         load.wait()
-    forward(0, MARGIN, rows - MARGIN)
-    receive(0)
-    forward(0, 0, MARGIN)
-    forward(0, rows - MARGIN, rows)
-    send(1)
-    receivers_at(1)
-    for moment in range(1, STEPS):
-        receive(moment)
-        forward(moment, 0, MARGIN)
-        forward(moment, rows - MARGIN, rows)
-        if moment + 1 < STEPS:
-            send(moment + 1)
-        forward(moment, MARGIN, rows - MARGIN)
-        receivers_at(moment + 1)
-    for load in loads[3:]:
-        load.wait()
-    for moment in range(STEPS, 0, -1):
-        slot = 2 * STEPS - moment
-        receive(slot)
-        backward(moment, 0, MARGIN)
-        backward(moment, rows - MARGIN, rows)
-        if moment > 1:
-            send(slot + 1)
-        backward(moment, MARGIN, rows - MARGIN)
-    for slot in range(2 * STEPS):
-        @pl.when(has_left)
-        def _():
-            copies[slot][0].wait_send()
-
-        @pl.when(has_right)
-        def _():
-            copies[slot][1].wait_send()
+    square(REACH, REACH + rows)
+    prepare(f0, MARGIN, hf0, 0, mf0, 0)
+    forward_inside(0)
+    for k in range(STEPS):
+        for s in range(shots):
+            receive(halos[k][s])
+            forward_point(k, 0, (s,))
+            forward_point(k, groups - 1, (s,))
+            if k + 1 < STEPS:
+                send(halos[k + 1][s])
+        if k + 1 < STEPS:
+            forward_product(k, 0)
+            forward_product(k, groups - 1)
+            forward_inside(k + 1)
+        sample(k)
+        send(samples[k])
+        if k == 0:
+            for load in loads[3:]:
+                load.wait()
+            prepare(a4, BORDER, ha, BORDER, ma0, BORDER)
+            receive(adj_halo)
+
+            @pl.loop(0, groups)
+            def _(g):
+                free_point(g)
+
+            send(border_halo)
+            receive(speed_halo)
+            square(0, REACH)
+            square(REACH + rows, 2 * REACH + rows)
+        if k > 0:
+            receive(samples[k - 1])
+            misfits(k - 1, True)
+            land(k - 1, {1: 0, 2: REACH, 3: REACH}[k])
+
+    sent(border_halo)
+    misfits(STEPS - 1, False)
+    sweep(0, groups, lambda g: drop_point(g, True), lambda g: adj_product(3, g))
+    backward(3, 1, groups - 1, True)
+    receive(samples[STEPS - 1])
+    misfits(STEPS - 1, True)
+    receive(border_halo)
+    edge = BORDER // group
+    sweep(-edge, 0, lambda g: drop_point(g, False), lambda g: adj_product(3, g))
+    sweep(
+        groups,
+        groups + edge,
+        lambda g: drop_point(g, False),
+        lambda g: adj_product(3, g),
+    )
+    edge -= 1
+    backward(3, -edge, 0, False)
+    backward(3, groups, groups + edge, False)
+    for g in (0, groups - 1):
+        backward_point(3, g, True)
+        adj_product(2, g)
+    edge -= 1
+    for g in (-1, groups):
+        backward_point(2, g, False)
+        adj_product(1, g)
+    backward(2, 0, groups, True)
+    backward(1, 0, groups, True)
+    for copies in pairs:
+        if copies is not border_halo:
+            sent(copies)
 
 
 def shot_gradient(
@@ -311,34 +585,50 @@
 ):
     shots, rows, depth, width = now.shape
     receivers = record_cells.shape[1]
-    chunk = 8
-    span = chunk * depth
     hbm = pl.BlockSpec(memory_space=pl.ANY)
     vmem = pl.BlockSpec(memory_space=pltpu.VMEM)
     smem = pl.BlockSpec(memory_space=pltpu.SMEM)
-    f32 = jnp.float32
+    f32, bf16 = jnp.float32, jnp.bfloat16
+    group = MARGIN
+    wide = rows + 2 * REACH
+    widest = rows + 2 * BORDER
+    exchanges = STEPS * shots + 3 + STEPS
     return pl.pallas_call(
         functools.partial(wave_kernel, lax.axis_size("dom")),
         out_shape=jax.ShapeDtypeStruct((rows, depth, width), f32),
         in_specs=[hbm] * 5 + [smem] * 3 + [vmem] * 2,
         out_specs=vmem,
-        scratch_shapes=[
-            pltpu.VMEM((2 * STEPS + 1, shots, rows + 2 * MARGIN, depth, width), f32),
+        scratch_shapes=[pltpu.VMEM((shots, rows + 2 * MARGIN, depth, width), f32)] * (STEPS + 1)
+        + [pltpu.VMEM((shots, widest, depth, width), f32)] * STEPS
+        + [
             pltpu.VMEM((shots, rows, depth, width), f32),
             pltpu.VMEM((shots, rows, depth, width), f32),
-            pltpu.VMEM((rows, depth, width), f32),
+            pltpu.VMEM((wide, depth, width), f32),
+            pltpu.VMEM((wide, depth, width), f32),
             pltpu.VMEM((STEPS, shots, rows, depth, width), f32),
             pltpu.VMEM((shots, rows, depth, width), f32),
-            pltpu.VMEM((STEPS, shots, rows, depth, width), f32),
-            pltpu.VMEM((shots, rows // chunk, receivers, span), jnp.bfloat16),
-            pltpu.VMEM((shots, rows // chunk, span, receivers), jnp.bfloat16),
+            pltpu.VMEM((shots, rows, depth, width), f32),
+            pltpu.VMEM((shots, widest, depth, width), f32),
+            pltpu.VMEM((shots, widest, depth, width), f32),
+            pltpu.VMEM((shots, rows, depth, 2 * width), bf16),
+            pltpu.VMEM((shots, rows, depth, 2 * width), bf16),
+            pltpu.VMEM((shots, widest, depth, 2 * width), bf16),
+            pltpu.VMEM((2 * width, width), bf16),
+            pltpu.VMEM((group * depth, 2 * group * depth), bf16),
+            pltpu.VMEM((shots, rows, depth, width), f32),
+            pltpu.VMEM((STEPS - 1, shots, wide, depth, width), f32),
+            pltpu.VMEM((shots, receivers, rows * depth), bf16),
+            pltpu.VMEM((shots, widest * depth, receivers), bf16),
             pltpu.VMEM((shots, receivers, width), f32),
             pltpu.VMEM((shots, receivers, width), f32),
-            pltpu.VMEM((receivers, 2 * width), f32),
+            pltpu.VMEM((STEPS, 8, width), f32),
+            pltpu.VMEM((STEPS, 8, width), f32),
+            pltpu.VMEM((STEPS, 2, 8, width), f32),
+            pltpu.VMEM((shots, receivers, 2 * width), bf16),
             pltpu.VMEM((rows, depth, width), f32),
             pltpu.SemaphoreType.DMA((5,)),
-            pltpu.SemaphoreType.DMA((2 * STEPS, 2)),
-            pltpu.SemaphoreType.DMA((2 * STEPS, 2)),
+            pltpu.SemaphoreType.DMA((exchanges, 2)),
+            pltpu.SemaphoreType.DMA((exchanges, 2)),
         ],
         compiler_params=pltpu.CompilerParams(
             collective_id=0, has_side_effects=True, vmem_limit_bytes=56 * 1024 * 1024

time: 71.6 us -> 62.2 us (0.87)
  Pallas kernels: 68.6 us -> 59.3 us
    pallas_call x1, Pallas kernels: 44.7 us -> 35.6 us  [shot_gradient(): pl.pallas_call(functools.partial(wave_kernel, lax.axis_size('dom')), out_...]
where the time goes in v1:
time: 62.2 us; the launch traced here: 62 us
  Pallas kernels  59.3 us (95%)
  local copies, waits for them, and re-layouts  1.05 us (2%)
  other arithmetic  1 us (2%)
  between operations  0.72 us (1%)
    pallas_call x1, Pallas kernels, shot_gradient(): pl.pallas_call(functools.partial(wave_kernel, lax.axis_size('dom')), out_...  35.6 us
    pallas_call x1, Pallas kernels, shared_update(): pl.pallas_call(functools.partial(shared_kernel, shots, doms), out_shape=j...  23.6 us

profile of v1, /device:TPU:0, one launch (start us, length us, event | category | flops | bytes accessed | tf_op | source)
XLA Modules:
  0.0 62.0 jit_solution(16693942557249985711)
XLA Ops:
  0.0 0.0 copy-start.2
  0.0 0.0 copy-start.3
  0.0 0.0 copy-start.4
  0.0 0.0 copy-start.1
  0.0 35.6 %shard_map.145 = f32[32,32,128]{2,1,0:T(8,128)} custom-call(f32[2,32,32,128]{3,2,1,0:T(8,128)} %now_hbm.1, f32[2,32,32,128]{3,2,1,0:T(8,128)} %adj_hbm.1, f32[2,32,32,128]{3,2,1,0:T(8,128)} %prev_hbm.1, f32[2,32,32,128]{3,2,1,0:T(8,128)} %later_hbm.1, f32[32,32,128]{2,1,0:T(8,128)} %speed_hbm.1, f32[2,4]{1,0:T(2,128)} %pulse.1, s32[2,8]{1,0:T(2,128)} %src_cells.1, ...), custom_call_target="tpu_custom_call" | custom-call | tf_op jit(solution)/shard_map/pallas_call | solution.py:596
  36.3 0.0 copy-done.2
  36.3 0.0 copy-done.3
  36.3 0.0 copy-done.4
  36.3 0.0 copy-done.1
  36.3 0.0 copy-start
  36.3 1.0 %copy-done = f32[32,32,128]{2,1,0:T(8,128)S(1)} copy-done((f32[32,32,128]{2,1,0:T(8,128)S(1)}, f32[32,32,128]{2,1,0:T(8,128)}, u32[]{:S(2)}) %copy-start) | copy-done | bytes 524312
  37.4 0.0 copy-start.5
  37.4 23.6 %shard_map.146 = f32[1024,128]{1,0:T(8,128)S(1)} custom-call(f32[1024,128]{1,0:T(8,128)S(1)} %bitcast.3, f32[1024,128]{1,0:T(8,128)S(1)} %bitcast.5, f32[256,256]{1,0:T(8,128)S(1)} %copy-done.2, f32[256,256]{1,0:T(8,128)S(1)} %copy-done.3, f32[256,1]{1,0:T(8,128)S(1)} %copy-done.4, f32[1]{0:T(128)S(6)} %copy.16.step_size), custom_call_target="tpu_custom_call" | custom-call | tf_op jit(solution)/shard_map/pallas_call | solution.py:836
  61.0 0.0 copy-done.5
  61.0 1.0 %slice_add_fusion = f32[32,32,32]{2,1,0:T(8,128)} fusion(f32[32,32,128]{2,1,0:T(8,128)S(1)} %bitcast.4, f32[32,32,128]{2,1,0:T(8,128)S(1)} %copy-done.5, s32[]{:T(128)S(6)} %select_n.3), kind=kLoop, calls=%fused_computation | loop fusion | flops 32768 | bytes 393220 | tf_op jit(solution)/shard_map/add | solution.py:900
Async XLA Ops:
  0.0 36.3 %copy-start.2 = (f32[256,256]{1,0:T(8,128)S(1)}, f32[256,256]{1,0:T(8,128)}, u32[]{:S(2)}) copy-start(f32[256,256]{1,0:T(8,128)} %constant.17.clone.basis) | copy-start | bytes 786436
  0.0 36.3 %copy-start.3 = (f32[256,256]{1,0:T(8,128)S(1)}, f32[256,256]{1,0:T(8,128)}, u32[]{:S(2)}) copy-start(f32[256,256]{1,0:T(8,128)} %constant.18.clone.basis_t) | copy-start | bytes 786436
  0.0 36.3 %copy-start.4 = (f32[256,1]{1,0:T(8,128)S(1)}, f32[256,1]{1,0:T(8,128)}, u32[]{:S(2)}) copy-start(f32[256,1]{1,0:T(8,128)} %constant.19.clone.gain) | copy-start | bytes 3076
  0.0 36.3 %copy-start.1 = (f32[32,32,128]{2,1,0:T(8,128)S(1)}, f32[32,32,128]{2,1,0:T(8,128)}, u32[]{:S(2)}) copy-start(f32[32,32,128]{2,1,0:T(8,128)} %param.16) | copy-start | bytes 1572868
  36.3 1.0 %copy-start = (f32[32,32,128]{2,1,0:T(8,128)S(1)}, f32[32,32,128]{2,1,0:T(8,128)}, u32[]{:S(2)}) copy-start(f32[32,32,128]{2,1,0:T(8,128)} %shard_map.145) | copy-start | bytes 1572868
  37.4 23.7 %copy-start.5 = (f32[32,32,128]{2,1,0:T(8,128)S(1)}, f32[32,32,128]{2,1,0:T(8,128)}, u32[]{:S(2)}) copy-start(f32[32,32,128]{2,1,0:T(8,128)} %speed_hbm.1) | copy-start | bytes 1572868

commit v2 on v1

--- a/solution.py
+++ b/solution.py
@@ -71,17 +71,15 @@
     speed,
     squares,
     laps,
-    mf0,
-    mf1,
-    ma0,
-    ma1,
     hf0,
     hf1,
     ha,
+    hb,
     across_y,
+    mixed,
+    blend,
     across_z,
     spread_src,
-    landed,
     pick,
     put,
     hot,
@@ -96,7 +94,7 @@
     recv_sem,
 ):
     fields = (f0, f1, f2, f3, f4)
-    mf, hf, ma = (mf0, mf1), (hf0, hf1), (ma0, ma1)
+    hf = (hf0, hf1)
     shots, rows, depth, width = prev.shape
     here = lax.axis_index("dom")
     left = jnp.maximum(here - 1, 0)
@@ -316,20 +314,24 @@
         ref[s, row, part, 0:width] = high
         ref[s, row, part, width : 2 * width] = low
 
-    def product(split, split_row, target, target_row):
+    everyone = tuple(range(shots))
+
+    def mix(split, row, mixed):
         lines = [
-            split[s, pl.ds(split_row, group)].reshape(group * depth, 2 * width)
-            for s in range(shots)
+            split[s, pl.ds(row, group)].reshape(group * depth, 2 * width) for s in everyone
         ]
         highs = jnp.concatenate([line[:, :width] for line in lines], axis=1)
         lows = jnp.concatenate([line[:, width:] for line in lines], axis=1)
         down = jnp.dot(
             across_z[...], jnp.concatenate([highs, lows], axis=0), preferred_element_type=f32
         )
-        for s in range(shots):
-            over = jnp.dot(lines[s], across_y[...], preferred_element_type=f32)
-            both = over + down[:, s * width : (s + 1) * width]
-            target[s, pl.ds(target_row, group)] = both.reshape(group, depth, width)
+        over = jnp.dot(
+            jnp.concatenate(lines, axis=0), across_y[...], preferred_element_type=f32
+        )
+        for s in everyone:
+            both = over[s * group * depth : (s + 1) * group * depth]
+            both = both + down[:, s * width : (s + 1) * width]
+            mixed[s, pl.ds(row, group)] = both.reshape(group, depth, width)
 
     def beside_x(window, i):
         summed = WEIGHTS[1] * (window[i + 3] + window[i + 5])
@@ -337,15 +339,13 @@
             summed += WEIGHTS[r] * (window[i + MARGIN + r] + window[i + MARGIN - r])
         return summed
 
-    def sweep(first, last, point, product_of):
-        point(first)
-
-        @pl.loop(first + 1, last)
+    def sweep(first, last, point, ahead):
+        ahead(first)
+
+        @pl.loop(first, last, unroll=2)
         def _(g):
-            product_of(g - 1)
             point(g)
-
-        product_of(last - 1)
+            ahead(g + 1)
 
     def square(first, last):
         @pl.loop(first, last)
@@ -353,21 +353,12 @@
             squares[x] = (COURANT / SCALE) * speed[x] * speed[x]
 
     parts = [pl.ds(h * half, half) for h in range(halves)]
-
-    def prepare(field, margin, split, split_margin, target, target_margin):
-        def point(g):
+    def prepare(field, margin, split, split_margin):
+        @pl.loop(0, rows)
+        def _(x):
             for s in range(shots):
-                for i in range(group):
-                    for part in parts:
-                        x = g * group + i
-                        keep_split(split, s, x + split_margin, part, field[s, x + margin, part])
-
-        sweep(
-            0,
-            groups,
-            point,
-            lambda g: product(split, g * group + split_margin, target, g * group + target_margin),
-        )
+                for part in parts:
+                    keep_split(split, s, x + split_margin, part, field[s, x + margin, part])
 
     def forward_point(k, g, which):
         x = g * group
@@ -376,7 +367,7 @@
             for s in which:
                 window = [field[s, x + i, part] for i in range(group + 2 * MARGIN)]
                 for i in range(group):
-                    lap = mf[k % 2][s, x + i, part] + beside_x(window, i)
+                    lap = beside_x(window, i) + mixed[s, x + i, part]
                     laps[k, s, x + i, part] = lap
                     if k == 0:
                         before = prev[s, x + i, part]
@@ -388,16 +379,10 @@
                     target[s, x + i + MARGIN, part] = fresh
                     keep_split(split, s, x + i, part, fresh)
 
-    def forward_product(k, g):
-        product(hf[(k + 1) % 2], g * group, mf[(k + 1) % 2], g * group)
-
     def forward_inside(k):
-        sweep(
-            1,
-            groups - 1,
-            lambda g: forward_point(k, g, range(shots)),
-            lambda g: forward_product(k, g) if k + 1 < STEPS else None,
-        )
+        ahead = lambda g: mix(hf[k % 2], g * group, mixed)
+        ahead(0)
+        sweep(1, groups - 1, lambda g: forward_point(k, g, everyone), ahead)
 
     def sample(k):
         split = hf[(k + 1) % 2]
@@ -427,19 +412,15 @@
                     at = s * tiles + t
                     block.append(missed[:, at : at + 1] * hot[s, pl.ds(t * 8, 8)])
                 high, low = split_two(jnp.concatenate(block, axis=0))
-                values[s, pl.ds(j * 8, 16), 0:width] = high
-                values[s, pl.ds(j * 8, 16), width : 2 * width] = low
-
-    def dropped(s, x, count):
+                values[k, s, pl.ds(j * 8, 16), 0:width] = high
+                values[k, s, pl.ds(j * 8, 16), width : 2 * width] = low
+
+    def dropped(k, s, x):
         at = pl.multiple_of((x + BORDER) * depth, group * depth)
-        both = jnp.dot(put[s, pl.ds(at, count * depth)], values[s], preferred_element_type=f32)
-        return (both[:, :width] + both[:, width:]).reshape(count, depth, width)
-
-    def land(k, extra):
-        @pl.loop(-extra // 8, (rows + extra) // 8)
-        def _(c):
-            for s in range(shots):
-                landed[k, s, pl.ds(c * 8 + REACH, 8)] = dropped(s, c * 8, 8)
+        both = jnp.dot(
+            put[s, pl.ds(at, group * depth)], values[k, s], preferred_element_type=f32
+        )
+        return (both[:, :width] + both[:, width:]).reshape(group, depth, width)
 
     def free_point(g):
         x = g * group
@@ -449,7 +430,7 @@
                     a4[s, x + BORDER - MARGIN + i, part] for i in range(group + 2 * MARGIN)
                 ]
                 for i in range(group):
-                    lap = ma0[s, x + i + BORDER, part] + beside_x(window, i)
+                    lap = beside_x(window, i) + blend[s, x + BORDER + i, part]
                     fresh = 2.0 * window[i + MARGIN] - later[s, x + i, part]
                     a3[s, x + i + BORDER, part] = fresh + squares[x + i + REACH, part] * lap
 
@@ -457,11 +438,11 @@
         x = g * group
         gathered = None
         for s in range(shots):
-            fresh = a3[s, pl.ds(x + BORDER, group)] + dropped(s, x, group)
+            fresh = a3[s, pl.ds(x + BORDER, group)] + dropped(STEPS - 1, s, x)
             a3[s, pl.ds(x + BORDER, group)] = fresh
             high, low = split_two(fresh)
-            ha[s, pl.ds(x + BORDER, group), :, 0:width] = high
-            ha[s, pl.ds(x + BORDER, group), :, width : 2 * width] = low
+            hb[s, pl.ds(x + BORDER, group), :, 0:width] = high
+            hb[s, pl.ds(x + BORDER, group), :, width : 2 * width] = low
             if inside:
                 term = fresh * laps[STEPS - 1, s, pl.ds(x, group)]
                 gathered = term if gathered is None else gathered + term
@@ -469,28 +450,27 @@
             total[pl.ds(x, group)] = gathered
 
     adj = {4: a4, 3: a3, 2: a2, 1: a1}
-    adj_mix = {4: ma0, 3: ma1, 2: ma0, 1: ma1}
-
-    def adj_product(m, g):
-        product(ha, g * group + BORDER, adj_mix[m], g * group + BORDER)
+    splits = {4: ha, 3: hb, 2: ha, 1: hb}
 
     def backward_point(m, g, inside):
         x = g * group
         field, after = adj[m], adj[m + 1]
-        for part in parts:
+        fallen = [dropped(m - 1, s, x) for s in range(shots)]
+        for h, part in enumerate(parts):
+            rim = slice(h * half, (h + 1) * half)
             gathered = [None] * group
             for s in range(shots):
                 window = [
                     field[s, x + BORDER - MARGIN + i, part] for i in range(group + 2 * MARGIN)
                 ]
                 for i in range(group):
-                    lap = adj_mix[m][s, x + i + BORDER, part] + beside_x(window, i)
+                    lap = beside_x(window, i) + blend[s, x + BORDER + i, part]
                     fresh = 2.0 * window[i + MARGIN] - after[s, x + i + BORDER, part]
-                    fresh = fresh + landed[m - 1, s, x + i + REACH, part]
+                    fresh = fresh + fallen[s][i, rim]
                     fresh = fresh + squares[x + i + REACH, part] * lap
                     if m > 1:
                         adj[m - 1][s, x + i + BORDER, part] = fresh
-                        keep_split(ha, s, x + i + BORDER, part, fresh)
+                        keep_split(splits[m - 1], s, x + i + BORDER, part, fresh)
                     if inside:
                         term = fresh * laps[m - 1, s, x + i, part]
                         gathered[i] = term if gathered[i] is None else gathered[i] + term
@@ -504,75 +484,67 @@
                         out[x + i, part] = factor * summed
 
     def backward(m, first, last, inside):
-        sweep(
-            first,
-            last,
-            lambda g: backward_point(m, g, inside),
-            lambda g: adj_product(m - 1, g) if m > 1 else None,
-        )
+        ahead = lambda g: mix(splits[m], g * group + BORDER, blend)
+        sweep(first, last, lambda g: backward_point(m, g, inside), ahead)
 
     for load in loads[:3]:
         load.wait()
     square(REACH, REACH + rows)
-    prepare(f0, MARGIN, hf0, 0, mf0, 0)
+    prepare(f0, MARGIN, hf0, 0)
     forward_inside(0)
     for k in range(STEPS):
-        for s in range(shots):
+        rims = (0, groups - 1)
+        for s in everyone:
             receive(halos[k][s])
-            forward_point(k, 0, (s,))
-            forward_point(k, groups - 1, (s,))
+            for g in rims:
+                forward_point(k, g, (s,))
             if k + 1 < STEPS:
                 send(halos[k + 1][s])
         if k + 1 < STEPS:
-            forward_product(k, 0)
-            forward_product(k, groups - 1)
             forward_inside(k + 1)
         sample(k)
         send(samples[k])
         if k == 0:
             for load in loads[3:]:
                 load.wait()
-            prepare(a4, BORDER, ha, BORDER, ma0, BORDER)
+            prepare(a4, BORDER, ha, BORDER)
             receive(adj_halo)
-
-            @pl.loop(0, groups)
-            def _(g):
-                free_point(g)
-
+            sweep(0, groups, free_point, lambda g: mix(ha, g * group + BORDER, blend))
             send(border_halo)
             receive(speed_halo)
             square(0, REACH)
             square(REACH + rows, 2 * REACH + rows)
-        if k > 0:
+        else:
             receive(samples[k - 1])
             misfits(k - 1, True)
-            land(k - 1, {1: 0, 2: REACH, 3: REACH}[k])
 
     sent(border_halo)
     misfits(STEPS - 1, False)
-    sweep(0, groups, lambda g: drop_point(g, True), lambda g: adj_product(3, g))
+
+    @pl.loop(0, groups, unroll=2)
+    def _(g):
+        drop_point(g, True)
+
     backward(3, 1, groups - 1, True)
     receive(samples[STEPS - 1])
     misfits(STEPS - 1, True)
     receive(border_halo)
-    edge = BORDER // group
-    sweep(-edge, 0, lambda g: drop_point(g, False), lambda g: adj_product(3, g))
-    sweep(
-        groups,
-        groups + edge,
-        lambda g: drop_point(g, False),
-        lambda g: adj_product(3, g),
-    )
-    edge -= 1
-    backward(3, -edge, 0, False)
-    backward(3, groups, groups + edge, False)
-    for g in (0, groups - 1):
-        backward_point(3, g, True)
-        adj_product(2, g)
-    edge -= 1
+    far = BORDER // group
+    for g in range(far):
+        drop_point(-1 - g, False)
+        drop_point(groups + g, False)
+    outer = [g for t in range(far - 1) for g in (-1 - t, groups + t)]
+    reached = outer + [0, groups - 1]
+    for g in reached[:2]:
+        mix(splits[3], g * group + BORDER, blend)
+    for n, g in enumerate(reached):
+        backward_point(3, g, g not in outer)
+        if n + 2 < len(reached):
+            mix(splits[3], reached[n + 2] * group + BORDER, blend)
+    for g in (-1, groups):
+        mix(splits[2], g * group + BORDER, blend)
     for g in (-1, groups):
         backward_point(2, g, False)
-        adj_product(1, g)
     backward(2, 0, groups, True)
     backward(1, 0, groups, True)
     for copies in pairs:
@@ -606,17 +578,15 @@
             pltpu.VMEM((wide, depth, width), f32),
             pltpu.VMEM((wide, depth, width), f32),
             pltpu.VMEM((STEPS, shots, rows, depth, width), f32),
-            pltpu.VMEM((shots, rows, depth, width), f32),
-            pltpu.VMEM((shots, rows, depth, width), f32),
-            pltpu.VMEM((shots, widest, depth, width), f32),
-            pltpu.VMEM((shots, widest, depth, width), f32),
             pltpu.VMEM((shots, rows, depth, 2 * width), bf16),
             pltpu.VMEM((shots, rows, depth, 2 * width), bf16),
             pltpu.VMEM((shots, widest, depth, 2 * width), bf16),
+            pltpu.VMEM((shots, widest, depth, 2 * width), bf16),
             pltpu.VMEM((2 * width, width), bf16),
+            pltpu.VMEM((shots, rows, depth, width), f32),
+            pltpu.VMEM((shots, widest, depth, width), f32),
             pltpu.VMEM((group * depth, 2 * group * depth), bf16),
             pltpu.VMEM((shots, rows, depth, width), f32),
-            pltpu.VMEM((STEPS - 1, shots, wide, depth, width), f32),
             pltpu.VMEM((shots, receivers, rows * depth), bf16),
             pltpu.VMEM((shots, widest * depth, receivers), bf16),
             pltpu.VMEM((shots, receivers, width), f32),
@@ -624,7 +594,7 @@
             pltpu.VMEM((STEPS, 8, width), f32),
             pltpu.VMEM((STEPS, 8, width), f32),
             pltpu.VMEM((STEPS, 2, 8, width), f32),
-            pltpu.VMEM((shots, receivers, 2 * width), bf16),
+            pltpu.VMEM((STEPS, shots, receivers, 2 * width), bf16),
             pltpu.VMEM((rows, depth, width), f32),
             pltpu.SemaphoreType.DMA((5,)),
             pltpu.SemaphoreType.DMA((exchanges, 2)),

time: 62.2 us -> 56.7 us (0.912)
  Pallas kernels: 59.3 us -> 53.7 us
    pallas_call x1, Pallas kernels: 35.6 us -> 30.9 us  [shot_gradient(): pl.pallas_call(functools.partial(wave_kernel, lax.axis_size('dom')), out_...]
    pallas_call x1, Pallas kernels: 23.6 us -> 22.8 us  [shared_update(): pl.pallas_call(functools.partial(shared_kernel, shots, doms), out_shape=j...]
where the time goes in v2:
time: 56.7 us; the launch traced here: 56.5 us
  Pallas kernels  53.7 us (95%)
  local copies, waits for them, and re-layouts  1.05 us (2%)
  other arithmetic  1 us (2%)
  between operations  0.72 us (1%)
    pallas_call x1, Pallas kernels, shot_gradient(): pl.pallas_call(functools.partial(wave_kernel, lax.axis_size('dom')), out_...  30.9 us
    pallas_call x1, Pallas kernels, shared_update(): pl.pallas_call(functools.partial(shared_kernel, shots, doms), out_shape=j...  22.8 us

profile of v2, /device:TPU:0, one launch (start us, length us, event | category | flops | bytes accessed | tf_op | source)
XLA Modules:
  0.0 56.5 jit_solution(3822743259502932777)
XLA Ops:
  0.0 0.0 copy-start.2
  0.0 0.0 copy-start.3
  0.0 0.0 copy-start.4
  0.0 0.0 copy-start.1
  0.0 30.9 %shard_map.145 = f32[32,32,128]{2,1,0:T(8,128)} custom-call(f32[2,32,32,128]{3,2,1,0:T(8,128)} %now_hbm.1, f32[2,32,32,128]{3,2,1,0:T(8,128)} %adj_hbm.1, f32[2,32,32,128]{3,2,1,0:T(8,128)} %prev_hbm.1, f32[2,32,32,128]{3,2,1,0:T(8,128)} %later_hbm.1, f32[32,32,128]{2,1,0:T(8,128)} %speed_hbm.1, f32[2,4]{1,0:T(2,128)} %pulse.1, s32[2,8]{1,0:T(2,128)} %src_cells.1, ...), custom_call_target="tpu_custom_call" | custom-call | tf_op jit(solution)/shard_map/pallas_call | solution.py:568
  31.5 0.0 copy-done.2
  31.6 0.0 copy-done.3
  31.6 0.0 copy-done.4
  31.6 0.0 copy-done.1
  31.6 0.0 copy-start
  31.6 1.0 %copy-done = f32[32,32,128]{2,1,0:T(8,128)S(1)} copy-done((f32[32,32,128]{2,1,0:T(8,128)S(1)}, f32[32,32,128]{2,1,0:T(8,128)}, u32[]{:S(2)}) %copy-start) | copy-done | bytes 524312
  32.6 0.0 copy-start.5
  32.6 22.8 %shard_map.146 = f32[1024,128]{1,0:T(8,128)S(1)} custom-call(f32[1024,128]{1,0:T(8,128)S(1)} %bitcast.3, f32[1024,128]{1,0:T(8,128)S(1)} %bitcast.5, f32[256,256]{1,0:T(8,128)S(1)} %copy-done.2, f32[256,256]{1,0:T(8,128)S(1)} %copy-done.3, f32[256,1]{1,0:T(8,128)S(1)} %copy-done.4, f32[1]{0:T(128)S(6)} %copy.16.step_size), custom_call_target="tpu_custom_call" | custom-call | tf_op jit(solution)/shard_map/pallas_call | solution.py:806
  55.4 0.0 copy-done.5
  55.5 1.0 %slice_add_fusion = f32[32,32,32]{2,1,0:T(8,128)} fusion(f32[32,32,128]{2,1,0:T(8,128)S(1)} %bitcast.4, f32[32,32,128]{2,1,0:T(8,128)S(1)} %copy-done.5, s32[]{:T(128)S(6)} %select_n.3), kind=kLoop, calls=%fused_computation | loop fusion | flops 32768 | bytes 393220 | tf_op jit(solution)/shard_map/add | solution.py:870
Async XLA Ops:
  0.0 31.5 %copy-start.2 = (f32[256,256]{1,0:T(8,128)S(1)}, f32[256,256]{1,0:T(8,128)}, u32[]{:S(2)}) copy-start(f32[256,256]{1,0:T(8,128)} %constant.17.clone.basis) | copy-start | bytes 786436
  0.0 31.6 %copy-start.3 = (f32[256,256]{1,0:T(8,128)S(1)}, f32[256,256]{1,0:T(8,128)}, u32[]{:S(2)}) copy-start(f32[256,256]{1,0:T(8,128)} %constant.18.clone.basis_t) | copy-start | bytes 786436
  0.0 31.6 %copy-start.4 = (f32[256,1]{1,0:T(8,128)S(1)}, f32[256,1]{1,0:T(8,128)}, u32[]{:S(2)}) copy-start(f32[256,1]{1,0:T(8,128)} %constant.19.clone.gain) | copy-start | bytes 3076
  0.0 31.6 %copy-start.1 = (f32[32,32,128]{2,1,0:T(8,128)S(1)}, f32[32,32,128]{2,1,0:T(8,128)}, u32[]{:S(2)}) copy-start(f32[32,32,128]{2,1,0:T(8,128)} %param.16) | copy-start | bytes 1572868
  31.6 1.0 %copy-start = (f32[32,32,128]{2,1,0:T(8,128)S(1)}, f32[32,32,128]{2,1,0:T(8,128)}, u32[]{:S(2)}) copy-start(f32[32,32,128]{2,1,0:T(8,128)} %shard_map.145) | copy-start | bytes 1572868
  32.6 22.8 %copy-start.5 = (f32[32,32,128]{2,1,0:T(8,128)S(1)}, f32[32,32,128]{2,1,0:T(8,128)}, u32[]{:S(2)}) copy-start(f32[32,32,128]{2,1,0:T(8,128)} %speed_hbm.1) | copy-start | bytes 1572868

commit v3 on v2

--- a/solution.py
+++ b/solution.py
@@ -44,8 +44,201 @@
     return band.astype(jnp.bfloat16)
 
 
-def wave_kernel(
+WAVE_REFS = 36
+
+
+class Prior:
+    def __init__(
+        self,
+        doms,
+        shares,
+        noise_hbm,
+        grad_map_hbm,
+        noise_map_hbm,
+        step_size,
+        out,
+        noise,
+        grad_map,
+        noise_map,
+        folded,
+        sums,
+        own,
+        noise_fold,
+        noise_lines,
+        grad_lines,
+        base,
+        update,
+        returned,
+        load_sem,
+        send_sem,
+        recv_sem,
+        shot_send,
+        shot_recv,
+    ):
+        self.doms, self.shares = doms, shares
+        self.noise, self.out, self.step_size = noise, out, step_size
+        self.grad_map, self.noise_map = grad_map, noise_map
+        self.folded, self.sums, self.own = folded, sums, own
+        self.noise_fold, self.noise_lines, self.grad_lines = noise_fold, noise_lines, grad_lines
+        self.base, self.update, self.returned = base, update, returned
+        self.me = lax.axis_index("shot")
+        self.here = lax.axis_index("dom")
+        self.depth = doms * shares
+        self.fold, self.rows, self.width = folded.shape[1:]
+        self.piece = self.width // shares
+        self.group = lax.broadcasted_iota(jnp.int32, (self.rows, self.width), 1) // self.piece
+        self.half = doms // 2
+        self.near = (self.here // self.half) * self.half
+        self.far = self.half - self.near
+        self.loads = [
+            pltpu.make_async_copy(noise_hbm, noise, load_sem.at[0]),
+            pltpu.make_async_copy(noise_map_hbm, noise_map, load_sem.at[1]),
+            pltpu.make_async_copy(grad_map_hbm, grad_map, load_sem.at[2]),
+        ]
+        turn = [lax.rem(self.here + o, self.half) for o in range(self.half)]
+        self.away = [self.far + t for t in turn]
+        self.close = [self.near + t for t in turn]
+        self.sems = (send_sem, recv_sem)
+        self.shot_sems = (shot_send, shot_recv)
+        self.moves = []
+
+    def load(self):
+        for load in self.loads:
+            load.start()
+
+    def slabs(self, source, level):
+        return [
+            source[pl.ds(block * self.fold + level, self.rows, stride=self.depth), :]
+            for block in range(self.shares)
+        ]
+
+    def join(self, slabs, share):
+        merged = None
+        for block in range(self.shares):
+            shift = (block - share) * self.piece
+            if isinstance(share, int):
+                shift = shift % self.width
+                turned = pltpu.roll(slabs[block], shift, 1) if shift else slabs[block]
+            else:
+                shift = lax.rem(shift + self.width, self.width)
+                turned = pltpu.roll(slabs[block], shift, 1)
+            merged = turned if merged is None else jnp.where(self.group == block, turned, merged)
+        return merged
+
+    def exchange(self, phase, source_of, target, far):
+        peers = self.away if far else self.close
+        for o in range(0 if far else 1, self.half):
+            index = o + (self.half if far else 0)
+            move = pltpu.make_async_remote_copy(
+                src_ref=source_of(peers[o]),
+                dst_ref=target.at[self.here],
+                send_sem=self.sems[0].at[phase, index],
+                recv_sem=self.sems[1].at[phase, index],
+                device_id={"dom": peers[o]},
+                device_id_type=MESH,
+            )
+            move.start()
+            self.moves.append((phase, move))
+
+    def arrive(self, phase):
+        for which, move in self.moves:
+            if which == phase:
+                move.wait_recv()
+
+    def send_noise(self):
+        for load in self.loads:
+            load.wait()
+
+        @pl.loop(0, self.fold)
+        def _(level):
+            self.noise_fold[level] = self.join(self.slabs(self.noise, level), self.me)
+
+        for far in (True, False):
+            self.exchange(0, lambda d: self.noise_fold.at[d], self.noise_lines, far)
+        self.noise_lines[self.here] = self.noise_fold[self.here]
+
+    def mapped(self, matrix, lines):
+        high, low = split_two(lines[...].reshape(self.doms * self.rows, self.width))
+        return jnp.dot(
+            matrix[...],
+            jnp.concatenate([high, low, high], axis=0),
+            preferred_element_type=jnp.float32,
+        )
+
+    def noise_update(self):
+        self.arrive(0)
+        root = jnp.sqrt(jnp.full((1, 1), self.step_size[0], jnp.float32))
+        self.base[...] = root * self.mapped(self.noise_map, self.noise_lines)
+
+    def apply(self, partial):
+        sharing = []
+        for far in (True, False):
+            start = self.far if far else self.near
+
+            @pl.loop(0, self.half)
+            def _(i):
+                slabs = self.slabs(partial, start + i)
+                for share in range(self.shares):
+                    self.folded[share, start + i] = self.join(slabs, share)
+
+            sharing.append([])
+            for o in range(1, self.shares):
+                peer = lax.rem(self.me + o, self.shares)
+                index = o + (self.shares if far else 0)
+                move = pltpu.make_async_remote_copy(
+                    src_ref=self.folded.at[peer, pl.ds(start, self.half)],
+                    dst_ref=self.sums.at[o, pl.ds(start, self.half)],
+                    send_sem=self.shot_sems[0].at[index],
+                    recv_sem=self.shot_sems[1].at[index],
+                    device_id={"shot": peer},
+                    device_id_type=MESH,
+                )
+                move.start()
+                sharing[-1].append(move)
+        for far in (True, False):
+            start = self.far if far else self.near
+            for move in sharing[0 if far else 1]:
+                move.wait_recv()
+            span = pl.ds(start, self.half)
+            gathered = self.folded[self.me, span]
+            for o in range(1, self.shares):
+                gathered = gathered + self.sums[o, span]
+            self.own[span] = gathered
+            self.exchange(1, lambda d: self.own.at[d], self.grad_lines, far)
+        self.grad_lines[self.here] = self.own[self.here]
+        self.arrive(1)
+        pull = self.mapped(self.grad_map, self.grad_lines)
+        fresh = self.base[...] - (0.5 * self.step_size[0]) * pull
+        self.update[...] = fresh.reshape(self.doms, self.rows, self.width)
+        for far in (True, False):
+            self.exchange(2, lambda d: self.update.at[d], self.returned, far)
+        self.returned[self.here] = self.update[self.here]
+        self.arrive(2)
+        for d in range(self.doms):
+            line = self.returned[d]
+            for block in range(self.shares):
+                shift = -block * self.piece % self.width
+                turned = pltpu.roll(line, shift, 1) if shift else line
+                self.out[pl.ds(block * self.fold + d, self.rows, stride=self.depth), :] = turned
+        for moves in sharing:
+            for move in moves:
+                move.wait_send()
+        for _, move in self.moves:
+            move.wait_send()
+
+
+def wave_kernel(doms, shares, *refs):
+    inputs = 14 if shares else 10
+    arrays, out, scratch = refs[:inputs], refs[inputs], refs[inputs + 1 :]
+    wave = arrays[:10] + (scratch[0] if shares else out,) + scratch[1:WAVE_REFS]
+    rest = arrays[10:] + (out,) + scratch[WAVE_REFS:] if shares else ()
+    gradient_steps(doms, shares, rest, *wave)
+
+
+def gradient_steps(
     doms,
+    shares,
+    rest,
     now_hbm,
     adj_hbm,
     prev_hbm,
@@ -118,16 +311,27 @@
         load.start()
 
     barrier = pltpu.get_barrier_semaphore()
-
-    @pl.when(has_left)
-    def _():
-        pl.semaphore_signal(barrier, inc=1, device_id={"dom": left}, device_id_type=MESH)
-
-    @pl.when(has_right)
-    def _():
-        pl.semaphore_signal(barrier, inc=1, device_id={"dom": right}, device_id_type=MESH)
-
-    pl.semaphore_wait(barrier, has_left.astype(jnp.int32) + has_right.astype(jnp.int32))
+    if shares:
+        prior = Prior(doms, shares, *rest)
+        prior.load()
+        for o in range(1, doms):
+            peer = {"dom": lax.rem(here + o, doms)}
+            pl.semaphore_signal(barrier, inc=1, device_id=peer, device_id_type=MESH)
+        for o in range(1, shares):
+            peer = {"shot": lax.rem(lax.axis_index("shot") + o, shares)}
+            pl.semaphore_signal(barrier, inc=1, device_id=peer, device_id_type=MESH)
+        pl.semaphore_wait(barrier, doms + shares - 2)
+    else:
+
+        @pl.when(has_left)
+        def _():
+            pl.semaphore_signal(barrier, inc=1, device_id={"dom": left}, device_id_type=MESH)
+
+        @pl.when(has_right)
+        def _():
+            pl.semaphore_signal(barrier, inc=1, device_id={"dom": right}, device_id_type=MESH)
+
+        pl.semaphore_wait(barrier, has_left.astype(jnp.int32) + has_right.astype(jnp.int32))
 
     pairs = []
 
@@ -481,7 +685,11 @@
                         total[x + i, part] = summed
                     else:
                         factor = (2.0 * COURANT / SCALE) * speed[x + i + REACH, part]
-                        out[x + i, part] = factor * summed
+                        if shares:
+                            line = pl.multiple_of((x + i) * depth + h * half, half)
+                            out[pl.ds(line, half), :] = factor * summed
+                        else:
+                            out[x + i, part] = factor * summed
 
     def backward(m, first, last, inside):
         ahead = lambda g: mix(splits[m], g * group + BORDER, blend)
@@ -517,6 +725,10 @@
         else:
             receive(samples[k - 1])
             misfits(k - 1, True)
+        if shares and k == 1:
+            prior.send_noise()
+        if shares and k == 2:
+            prior.noise_update()
 
     sent(border_halo)
     misfits(STEPS - 1, False)
@@ -547,13 +759,26 @@
         backward_point(2, g, False)
     backward(2, 0, groups, True)
     backward(1, 0, groups, True)
+    if shares:
+        prior.apply(out)
     for copies in pairs:
         if copies is not border_halo:
             sent(copies)
 
 
 def shot_gradient(
-    velocity, prev, now, later, adjoint, wavelet, source_cells, signs, record_cells, observed
+    velocity,
+    prev,
+    now,
+    later,
+    adjoint,
+    wavelet,
+    source_cells,
+    signs,
+    record_cells,
+    observed,
+    noise_field=None,
+    step_size=None,
 ):
     shots, rows, depth, width = now.shape
     receivers = record_cells.shape[1]
@@ -565,12 +790,44 @@
     wide = rows + 2 * REACH
     widest = rows + 2 * BORDER
     exchanges = STEPS * shots + 3 + STEPS
+    doms = lax.axis_size("dom")
+    shares = 0 if noise_field is None else lax.axis_size("shot")
+    more, more_specs, first, last = (), [], [], []
+    if shares:
+        lines = (doms, rows, width)
+        maps = (doms * rows, 3 * doms * rows)
+        more = (noise_field.reshape(rows * depth, width), *prior_maps(doms * rows), step_size)
+        more_specs = [hbm] * 3 + [smem]
+        first = [pltpu.VMEM((rows * depth, width), f32)]
+        last = [
+            pltpu.VMEM((rows * depth, width), f32),
+            pltpu.VMEM(maps, bf16),
+            pltpu.VMEM(maps, bf16),
+            pltpu.VMEM((shares, *lines), f32),
+            pltpu.VMEM((shares, *lines), f32),
+            pltpu.VMEM(lines, f32),
+            pltpu.VMEM(lines, f32),
+            pltpu.VMEM(lines, f32),
+            pltpu.VMEM(lines, f32),
+            pltpu.VMEM((doms * rows, width), f32),
+            pltpu.VMEM(lines, f32),
+            pltpu.VMEM(lines, f32),
+            pltpu.SemaphoreType.DMA((3,)),
+            pltpu.SemaphoreType.DMA((3, doms)),
+            pltpu.SemaphoreType.DMA((3, doms)),
+            pltpu.SemaphoreType.DMA((2 * shares,)),
+            pltpu.SemaphoreType.DMA((2 * shares,)),
+        ]
+    else:
+        first = [pltpu.VMEM((8, width), f32)]
+    shape = (rows * depth, width) if shares else (rows, depth, width)
     return pl.pallas_call(
-        functools.partial(wave_kernel, lax.axis_size("dom")),
-        out_shape=jax.ShapeDtypeStruct((rows, depth, width), f32),
-        in_specs=[hbm] * 5 + [smem] * 3 + [vmem] * 2,
+        functools.partial(wave_kernel, doms, shares),
+        out_shape=jax.ShapeDtypeStruct(shape, f32),
+        in_specs=[hbm] * 5 + [smem] * 3 + [vmem] * 2 + more_specs,
         out_specs=vmem,
-        scratch_shapes=[pltpu.VMEM((shots, rows + 2 * MARGIN, depth, width), f32)] * (STEPS + 1)
+        scratch_shapes=first
+        + [pltpu.VMEM((shots, rows + 2 * MARGIN, depth, width), f32)] * (STEPS + 1)
         + [pltpu.VMEM((shots, widest, depth, width), f32)] * STEPS
         + [
             pltpu.VMEM((shots, rows, depth, width), f32),
@@ -599,7 +856,8 @@
             pltpu.SemaphoreType.DMA((5,)),
             pltpu.SemaphoreType.DMA((exchanges, 2)),
             pltpu.SemaphoreType.DMA((exchanges, 2)),
-        ],
+        ]
+        + last,
         compiler_params=pltpu.CompilerParams(
             collective_id=0, has_side_effects=True, vmem_limit_bytes=56 * 1024 * 1024
         ),
@@ -614,7 +872,23 @@
         signs,
         record_cells,
         observed,
+        *more,
     )
+
+
+def prior_maps(length):
+    wave = np.arange(length)[:, None]
+    phase = wave * (2 * np.arange(length)[None, :] + 1) % (4 * length)
+    factor = np.where(wave == 0, math.sqrt(1.0 / length), math.sqrt(2.0 / length))
+    basis = factor * np.cos(math.pi / (2.0 * length) * phase)
+    gain = 1.0 / np.sqrt(1.0 + wave / (length // 32))
+    maps = []
+    for weights in (gain * gain, gain):
+        whole = basis.T @ (weights * basis)
+        high = whole.astype(jnp.bfloat16)
+        low = (whole - high.astype(np.float64)).astype(jnp.bfloat16)
+        maps.append(jnp.asarray(np.concatenate([high, high, low], axis=1)))
+    return maps
 
 
 def cosine_basis(length):
@@ -643,197 +917,6 @@
     weights = spectrum * (-0.5 * rate * spectrum * grad_hat + jnp.sqrt(rate) * noise_hat)
     update = lax.dot_general(basis, weights, (((0,), (0,)), ((), ())), precision=highest)
     return update.reshape(gradient.shape)
-
-
-def shared_kernel(
-    shots,
-    doms,
-    partial,
-    noise,
-    basis,
-    basis_t,
-    gain,
-    step_size,
-    out,
-    folded,
-    noise_fold,
-    sums,
-    own,
-    noise_lines,
-    grad_lines,
-    update,
-    returned,
-    send_sem,
-    recv_sem,
-    shot_send,
-    shot_recv,
-):
-    depth, rows, width = shots * folded.shape[1], folded.shape[2], folded.shape[3]
-    fold = folded.shape[1]
-    lot = fold // doms
-    lane_share = width // shots
-    me = lax.axis_index("shot")
-    here = lax.axis_index("dom")
-    dom_peer = [lax.rem(here + o, doms) for o in range(doms)]
-    shot_peer = [lax.rem(me + o, shots) for o in range(shots)]
-
-    barrier = pltpu.get_barrier_semaphore()
-    for o in range(1, doms):
-        pl.semaphore_signal(barrier, inc=1, device_id={"dom": dom_peer[o]}, device_id_type=MESH)
-    for o in range(1, shots):
-        pl.semaphore_signal(barrier, inc=1, device_id={"shot": shot_peer[o]}, device_id_type=MESH)
-
-    group = lax.broadcasted_iota(jnp.int32, (rows, width), 1) // lane_share
-
-    def fold_lanes(source, target):
-        @pl.loop(0, fold)
-        def _(level):
-            slabs = [
-                source[pl.ds(block * fold + level, rows, stride=depth), :]
-                for block in range(shots)
-            ]
-            for share in range(shots):
-                merged = None
-                for block in range(shots):
-                    shift = (block - share) * lane_share % width
-                    turned = pltpu.roll(slabs[block], shift, 1) if shift else slabs[block]
-                    merged = turned if merged is None else jnp.where(group == block, turned, merged)
-                target[share, level] = merged
-
-    def exchange(phase, source_of, target):
-        moves = []
-        for o in range(1, doms):
-            moves.append(
-                pltpu.make_async_remote_copy(
-                    src_ref=source_of(dom_peer[o]),
-                    dst_ref=target.at[here],
-                    send_sem=send_sem.at[phase, o],
-                    recv_sem=recv_sem.at[phase, o],
-                    device_id={"dom": dom_peer[o]},
-                    device_id_type=MESH,
-                )
-            )
-        return moves
-
-    fold_lanes(partial, folded)
-    pl.semaphore_wait(barrier, doms + shots - 2)
-    sharing = []
-    for o in range(1, shots):
-        move = pltpu.make_async_remote_copy(
-            src_ref=folded.at[shot_peer[o]],
-            dst_ref=sums.at[o],
-            send_sem=shot_send.at[o],
-            recv_sem=shot_recv.at[o],
-            device_id={"shot": shot_peer[o]},
-            device_id_type=MESH,
-        )
-        move.start()
-        sharing.append(move)
-    fold_lanes(noise, noise_fold)
-    noise_moves = exchange(0, lambda d: noise_fold.at[me, pl.ds(d * lot, lot)], noise_lines)
-    for move in noise_moves:
-        move.start()
-    noise_lines[here] = noise_fold[me, pl.ds(here * lot, lot)]
-    for move in noise_moves:
-        move.wait_recv()
-    rate = step_size[0]
-    highest = lax.Precision.HIGHEST
-    lines = doms * rows
-    noise_hats = [
-        jnp.dot(
-            basis[...],
-            noise_lines[:, i].reshape(lines, width),
-            precision=highest,
-            preferred_element_type=jnp.float32,
-        )
-        for i in range(lot)
-    ]
-    root = jnp.sqrt(jnp.full((1, 1), rate, jnp.float32))
-    for move in sharing:
-        move.wait_recv()
-    gathered = folded[me]
-    for o in range(1, shots):
-        gathered = gathered + sums[o]
-    own[...] = gathered
-    grad_moves = exchange(1, lambda d: own.at[pl.ds(d * lot, lot)], grad_lines)
-    for move in grad_moves:
-        move.start()
-    grad_lines[here] = own[pl.ds(here * lot, lot)]
-    for move in grad_moves:
-        move.wait_recv()
-    for i in range(lot):
-        grad_hat = jnp.dot(
-            basis[...],
-            grad_lines[:, i].reshape(lines, width),
-            precision=highest,
-            preferred_element_type=jnp.float32,
-        )
-        weights = gain[...] * (-0.5 * rate * gain[...] * grad_hat + root * noise_hats[i])
-        update[:, i] = jnp.dot(
-            basis_t[...], weights, precision=highest, preferred_element_type=jnp.float32
-        ).reshape(doms, rows, width)
-    back_moves = exchange(2, lambda d: update.at[d], returned)
-    for move in back_moves:
-        move.start()
-    returned[here] = update[here]
-    for move in back_moves:
-        move.wait_recv()
-    for d in range(doms):
-        for i in range(lot):
-            line = returned[d, i]
-            for block in range(shots):
-                shift = -block * lane_share % width
-                turned = pltpu.roll(line, shift, 1) if shift else line
-                out[pl.ds(block * fold + d * lot + i, rows, stride=depth), :] = turned
-    for move in sharing + noise_moves + grad_moves + back_moves:
-        move.wait_send()
-
-
-def shared_update(partial_value, noise_field, step_size):
-    rows, depth, width = partial_value.shape
-    shots, doms = lax.axis_size("shot"), lax.axis_size("dom")
-    length = rows * doms
-    fold = depth // shots
-    lot = fold // doms
-    wave = np.arange(length)[:, None]
-    phase = wave * (2 * np.arange(length)[None, :] + 1) % (4 * length)
-    factor = np.where(wave == 0, math.sqrt(1.0 / length), math.sqrt(2.0 / length))
-    basis = (factor * np.cos(math.pi / (2.0 * length) * phase)).astype(np.float32)
-    gain = (1.0 / np.sqrt(1.0 + wave / (length // 32))).astype(np.float32)
-    f32 = jnp.float32
-    vmem = pl.BlockSpec(memory_space=pltpu.VMEM)
-    smem = pl.BlockSpec(memory_space=pltpu.SMEM)
-    result = pl.pallas_call(
-        functools.partial(shared_kernel, shots, doms),
-        out_shape=jax.ShapeDtypeStruct((rows * depth, width), f32),
-        in_specs=[vmem] * 5 + [smem],
-        out_specs=vmem,
-        scratch_shapes=[
-            pltpu.VMEM((shots, fold, rows, width), f32),
-            pltpu.VMEM((shots, fold, rows, width), f32),
-            pltpu.VMEM((shots, fold, rows, width), f32),
-            pltpu.VMEM((fold, rows, width), f32),
-            pltpu.VMEM((doms, lot, rows, width), f32),
-            pltpu.VMEM((doms, lot, rows, width), f32),
-            pltpu.VMEM((doms, lot, rows, width), f32),
-            pltpu.VMEM((doms, lot, rows, width), f32),
-            pltpu.SemaphoreType.DMA((3, doms)),
-            pltpu.SemaphoreType.DMA((3, doms)),
-            pltpu.SemaphoreType.DMA((shots,)),
-            pltpu.SemaphoreType.DMA((shots,)),
-        ],
-        compiler_params=pltpu.CompilerParams(
-            collective_id=1, has_side_effects=True, vmem_limit_bytes=32 * 1024 * 1024
-        ),
-    )(
-        partial_value.reshape(rows * depth, width),
-        noise_field.reshape(rows * depth, width),
-        jnp.asarray(basis),
-        jnp.asarray(np.ascontiguousarray(basis.T)),
-        jnp.asarray(gain),
-        step_size,
-    )
-    return result.reshape(rows, depth, width)[:, :, : width // shots]
 
 
 def body(
@@ -850,7 +933,7 @@
     record_cells,
     observed,
 ):
-    partial_value = shot_gradient(
+    fields = (
         velocity,
         field_prev,
         field_now,
@@ -863,11 +946,14 @@
         observed,
     )
     rate = step_size[0]
-    shot_rows = velocity.shape[2] // lax.axis_size("shot")
+    rows, depth, width = velocity.shape
+    shares = lax.axis_size("shot")
+    shot_rows = width // shares
     start = lax.axis_index("shot") * shot_rows
-    if velocity.shape[1] % (lax.axis_size("shot") * lax.axis_size("dom")) == 0:
-        moved = shared_update(partial_value, noise_field, step_size)
-        return lax.dynamic_slice_in_dim(velocity, start, shot_rows, 2) + moved
+    if depth == shares * lax.axis_size("dom"):
+        moved = shot_gradient(*fields, noise_field, step_size).reshape(velocity.shape)
+        return lax.dynamic_slice_in_dim(velocity, start, shot_rows, 2) + moved[:, :, :shot_rows]
+    partial_value = shot_gradient(*fields)
     share = lax.psum_scatter(partial_value, "shot", scatter_dimension=2, tiled=True)
     noise_part = lax.dynamic_slice_in_dim(noise_field, start, shot_rows, 2)
     grad_cols, noise_cols = (

time: 56.7 us -> 55.7 us (0.982)
  other arithmetic: 1 us -> 2.05 us
  local copies, waits for them, and re-layouts: 1.05 us -> 0.01 us
  Pallas kernels: 53.7 us -> 52.8 us
    unnamed x12 -> x2, local copies, waits for them, and re-layouts: 1.05 us -> 0.01 us
    add x1, other arithmetic: 1 us -> 2.05 us  [body(): lax.dynamic_slice_in_dim(velocity, start, shot_rows, 2)]
    pallas_call x2 -> x1, Pallas kernels: 53.7 us -> 52.8 us  [shot_gradient(): pl.pallas_call(functools.partial(wave_kernel, doms, shares), out_shape=ja...]
where the time goes in v3:
time: 55.7 us; the launch traced here: 55.5 us
  Pallas kernels  52.8 us (95%)
  other arithmetic  2.05 us (4%)
  between operations  0.68 us (1%)
    pallas_call x1, Pallas kernels, shot_gradient(): pl.pallas_call(functools.partial(wave_kernel, doms, shares), out_shape=ja...  52.8 us
    add x1, other arithmetic, body(): lax.dynamic_slice_in_dim(velocity, start, shot_rows, 2)  2.05 us

profile of v3, /device:TPU:0, one launch (start us, length us, event | category | flops | bytes accessed | tf_op | source)
XLA Modules:
  0.0 55.5 jit_solution(14685558176436913833)
XLA Ops:
  0.7 0.0 copy-start
  0.7 52.8 %shard_map.136 = f32[1024,128]{1,0:T(8,128)} custom-call(f32[2,32,32,128]{3,2,1,0:T(8,128)} %refs_0_.1, f32[2,32,32,128]{3,2,1,0:T(8,128)} %refs_1_.1, f32[2,32,32,128]{3,2,1,0:T(8,128)} %refs_2_.1, f32[2,32,32,128]{3,2,1,0:T(8,128)} %refs_3_.1, f32[32,32,128]{2,1,0:T(8,128)} %refs_4_.1, f32[2,4]{1,0:T(2,128)} %refs_5_.1, s32[2,8]{1,0:T(2,128)} %refs_6_.1, ...), custom_call_target="tpu_custom_call" | custom-call | tf_op jit(solution)/shard_map/pallas_call | solution.py:824
  53.5 0.0 copy-done
  53.5 2.0 %slice_add_fusion = f32[32,32,32]{2,1,0:T(8,128)} fusion(f32[32,32,128]{2,1,0:T(8,128)} %bitcast.2, f32[32,32,128]{2,1,0:T(8,128)S(1)} %copy-done, s32[]{:T(128)S(6)} %select_n.3), kind=kLoop, calls=%fused_computation | loop fusion | flops 32768 | bytes 393220 | tf_op jit(solution)/shard_map/add | solution.py:955
Async XLA Ops:
  0.7 52.8 %copy-start = (f32[32,32,128]{2,1,0:T(8,128)S(1)}, f32[32,32,128]{2,1,0:T(8,128)}, u32[]{:S(2)}) copy-start(f32[32,32,128]{2,1,0:T(8,128)} %refs_4_.1) | copy-start | bytes 1572868

commit v4 on v3

--- a/solution.py
+++ b/solution.py
@@ -101,6 +101,7 @@
         self.sems = (send_sem, recv_sem)
         self.shot_sems = (shot_send, shot_recv)
         self.moves = []
+        self.sharing = []
 
     def load(self):
         for load in self.loads:
@@ -145,7 +146,7 @@
             if which == phase:
                 move.wait_recv()
 
-    def send_noise(self):
+    def fold_noise(self):
         for load in self.loads:
             load.wait()
 
@@ -153,6 +154,7 @@
         def _(level):
             self.noise_fold[level] = self.join(self.slabs(self.noise, level), self.me)
 
+    def send_noise(self):
         for far in (True, False):
             self.exchange(0, lambda d: self.noise_fold.at[d], self.noise_lines, far)
         self.noise_lines[self.here] = self.noise_fold[self.here]
@@ -170,34 +172,62 @@
         root = jnp.sqrt(jnp.full((1, 1), self.step_size[0], jnp.float32))
         self.base[...] = root * self.mapped(self.noise_map, self.noise_lines)
 
+    def slabs_part(self, source, level, first, count):
+        return [
+            source[
+                pl.ds(first * self.depth + block * self.fold + level, count, stride=self.depth), :
+            ]
+            for block in range(self.shares)
+        ]
+
+    def share_out(self, partial, part, first, count, start, levels):
+        group = self.group[:count]
+
+        @pl.loop(0, levels, unroll=2)
+        def _(i):
+            slabs = self.slabs_part(partial, start + i, first, count)
+            for share in range(self.shares):
+                merged = None
+                for block in range(self.shares):
+                    shift = (block - share) * self.piece % self.width
+                    turned = pltpu.roll(slabs[block], shift, 1) if shift else slabs[block]
+                    if merged is None:
+                        merged = turned
+                    else:
+                        merged = jnp.where(group == block, turned, merged)
+                self.folded[share, start + i, pl.ds(first, count)] = merged
+
+        moves = []
+        for o in range(1, self.shares):
+            peer = lax.rem(self.me + o, self.shares)
+            index = o + part * self.shares
+            span, lines = pl.ds(start, levels), pl.ds(first, count)
+            move = pltpu.make_async_remote_copy(
+                src_ref=self.folded.at[peer, span, lines],
+                dst_ref=self.sums.at[o, span, lines],
+                send_sem=self.shot_sems[0].at[index],
+                recv_sem=self.shot_sems[1].at[index],
+                device_id={"shot": peer},
+                device_id_type=MESH,
+            )
+            move.start()
+            moves.append(move)
+        self.sharing.append(moves)
+
+    def share_first(self, partial):
+        self.share_out(partial, 0, 0, self.rows // 2, 0, self.doms)
+
     def apply(self, partial):
-        sharing = []
+        rest = self.rows - self.rows // 2
+        self.share_out(partial, 1, self.rows // 2, rest, self.far, self.half)
+        self.share_out(partial, 2, self.rows // 2, rest, self.near, self.half)
+        self.noise_update()
+        sharing = self.sharing
+        for move in sharing[0]:
+            move.wait_recv()
         for far in (True, False):
             start = self.far if far else self.near
-
-            @pl.loop(0, self.half)
-            def _(i):
-                slabs = self.slabs(partial, start + i)
-                for share in range(self.shares):
-                    self.folded[share, start + i] = self.join(slabs, share)
-
-            sharing.append([])
-            for o in range(1, self.shares):
-                peer = lax.rem(self.me + o, self.shares)
-                index = o + (self.shares if far else 0)
-                move = pltpu.make_async_remote_copy(
-                    src_ref=self.folded.at[peer, pl.ds(start, self.half)],
-                    dst_ref=self.sums.at[o, pl.ds(start, self.half)],
-                    send_sem=self.shot_sems[0].at[index],
-                    recv_sem=self.shot_sems[1].at[index],
-                    device_id={"shot": peer},
-                    device_id_type=MESH,
-                )
-                move.start()
-                sharing[-1].append(move)
-        for far in (True, False):
-            start = self.far if far else self.near
-            for move in sharing[0 if far else 1]:
+            for move in sharing[1 if far else 2]:
                 move.wait_recv()
             span = pl.ds(start, self.half)
             gathered = self.folded[self.me, span]
@@ -410,12 +440,15 @@
         speed_hbm.at[pl.ds(rows - REACH, REACH)],
         speed.at[pl.ds(0, REACH)],
     )
-    border_halo = pair(
-        a3.at[:, pl.ds(BORDER, BORDER)],
-        a3.at[:, pl.ds(BORDER + rows, BORDER)],
-        a3.at[:, pl.ds(rows, BORDER)],
-        a3.at[:, pl.ds(0, BORDER)],
-    )
+    border_halos = [
+        pair(
+            a3.at[s, pl.ds(BORDER, BORDER)],
+            a3.at[s, pl.ds(BORDER + rows, BORDER)],
+            a3.at[s, pl.ds(rows, BORDER)],
+            a3.at[s, pl.ds(0, BORDER)],
+        )
+        for s in range(shots)
+    ]
     samples = [
         pair(found.at[k], beside.at[k, 1], found.at[k], beside.at[k, 0]) for k in range(STEPS)
     ]
@@ -708,29 +741,36 @@
                 forward_point(k, g, (s,))
             if k + 1 < STEPS:
                 send(halos[k + 1][s])
+        for s in everyone:
+            if k == (1 if 2 * s < shots else 2):
+                send(border_halos[s])
+        if k == 1:
+            sample(0)
+            send(samples[0])
         if k + 1 < STEPS:
             forward_inside(k + 1)
-        sample(k)
-        send(samples[k])
+        if k > 0:
+            sample(k)
+            send(samples[k])
         if k == 0:
             for load in loads[3:]:
                 load.wait()
             prepare(a4, BORDER, ha, BORDER)
             receive(adj_halo)
             sweep(0, groups, free_point, lambda g: mix(ha, g * group + BORDER, blend))
-            send(border_halo)
             receive(speed_halo)
             square(0, REACH)
             square(REACH + rows, 2 * REACH + rows)
         else:
             receive(samples[k - 1])
             misfits(k - 1, True)
-        if shares and k == 1:
-            prior.send_noise()
         if shares and k == 2:
-            prior.noise_update()
-
-    sent(border_halo)
+            prior.fold_noise()
+    if shares:
+        prior.send_noise()
+
+    for copies in border_halos:
+        sent(copies)
     misfits(STEPS - 1, False)
 
     @pl.loop(0, groups, unroll=2)
@@ -740,7 +780,8 @@
     backward(3, 1, groups - 1, True)
     receive(samples[STEPS - 1])
     misfits(STEPS - 1, True)
-    receive(border_halo)
+    for copies in border_halos:
+        receive(copies)
     far = BORDER // group
     for g in range(far):
         drop_point(-1 - g, False)
@@ -758,11 +799,14 @@
     for g in (-1, groups):
         backward_point(2, g, False)
     backward(2, 0, groups, True)
-    backward(1, 0, groups, True)
+    backward(1, 0, groups // 2, True)
+    if shares:
+        prior.share_first(out)
+    backward(1, groups // 2, groups, True)
     if shares:
         prior.apply(out)
     for copies in pairs:
-        if copies is not border_halo:
+        if not any(copies is other for other in border_halos):
             sent(copies)
 
 
@@ -789,7 +833,7 @@
     group = MARGIN
     wide = rows + 2 * REACH
     widest = rows + 2 * BORDER
-    exchanges = STEPS * shots + 3 + STEPS
+    exchanges = STEPS * shots + 2 + shots + STEPS
     doms = lax.axis_size("dom")
     shares = 0 if noise_field is None else lax.axis_size("shot")
     more, more_specs, first, last = (), [], [], []
@@ -815,8 +859,8 @@
             pltpu.SemaphoreType.DMA((3,)),
             pltpu.SemaphoreType.DMA((3, doms)),
             pltpu.SemaphoreType.DMA((3, doms)),
-            pltpu.SemaphoreType.DMA((2 * shares,)),
-            pltpu.SemaphoreType.DMA((2 * shares,)),
+            pltpu.SemaphoreType.DMA((3 * shares,)),
+            pltpu.SemaphoreType.DMA((3 * shares,)),
         ]
     else:
         first = [pltpu.VMEM((8, width), f32)]

time: 55.7 us -> 55.3 us (level)
  no operation moved by 1% of the time
where the time goes in v4:
time: 55.3 us; the launch traced here: 55.1 us
  Pallas kernels  52.4 us (95%)
  other arithmetic  2.05 us (4%)
  between operations  0.68 us (1%)
    pallas_call x1, Pallas kernels, shot_gradient(): pl.pallas_call(functools.partial(wave_kernel, doms, shares), out_shape=ja...  52.4 us
    add x1, other arithmetic, body(): lax.dynamic_slice_in_dim(velocity, start, shot_rows, 2)  2.05 us

profile of v4, /device:TPU:0, one launch (start us, length us, event | category | flops | bytes accessed | tf_op | source)
XLA Modules:
  0.0 55.1 jit_solution(7551027745981958035)
XLA Ops:
  0.7 0.0 copy-start
  0.7 52.4 %shard_map.136 = f32[1024,128]{1,0:T(8,128)} custom-call(f32[2,32,32,128]{3,2,1,0:T(8,128)} %refs_0_.1, f32[2,32,32,128]{3,2,1,0:T(8,128)} %refs_1_.1, f32[2,32,32,128]{3,2,1,0:T(8,128)} %refs_2_.1, f32[2,32,32,128]{3,2,1,0:T(8,128)} %refs_3_.1, f32[32,32,128]{2,1,0:T(8,128)} %refs_4_.1, f32[2,4]{1,0:T(2,128)} %refs_5_.1, s32[2,8]{1,0:T(2,128)} %refs_6_.1, ...), custom_call_target="tpu_custom_call" | custom-call | tf_op jit(solution)/shard_map/pallas_call | solution.py:868
  53.0 0.0 copy-done
  53.0 2.0 %slice_add_fusion = f32[32,32,32]{2,1,0:T(8,128)} fusion(f32[32,32,128]{2,1,0:T(8,128)} %bitcast.2, f32[32,32,128]{2,1,0:T(8,128)S(1)} %copy-done, s32[]{:T(128)S(6)} %select_n.3), kind=kLoop, calls=%fused_computation | loop fusion | flops 32768 | bytes 393220 | tf_op jit(solution)/shard_map/add | solution.py:999
Async XLA Ops:
  0.7 52.4 %copy-start = (f32[32,32,128]{2,1,0:T(8,128)S(1)}, f32[32,32,128]{2,1,0:T(8,128)}, u32[]{:S(2)}) copy-start(f32[32,32,128]{2,1,0:T(8,128)} %refs_4_.1) | copy-start | bytes 1572868

commit v5 on v4

--- a/solution.py
+++ b/solution.py
@@ -261,14 +261,23 @@
     inputs = 14 if shares else 10
     arrays, out, scratch = refs[:inputs], refs[inputs], refs[inputs + 1 :]
     wave = arrays[:10] + (scratch[0] if shares else out,) + scratch[1:WAVE_REFS]
-    rest = arrays[10:] + (out,) + scratch[WAVE_REFS:] if shares else ()
-    gradient_steps(doms, shares, rest, *wave)
+    small, scratch = scratch[WAVE_REFS : WAVE_REFS + 6], scratch[WAVE_REFS + 6 :]
+    staged = [
+        pltpu.make_async_copy(source, target, small[5].at[i])
+        for i, (source, target) in enumerate(zip(arrays[5:10], small))
+    ]
+    for copy in staged:
+        copy.start()
+    wave = wave[:5] + small[:5] + wave[10:]
+    rest = arrays[10:] + (out,) + scratch if shares else ()
+    gradient_steps(doms, shares, rest, staged, *wave)
 
 
 def gradient_steps(
     doms,
     shares,
     rest,
+    staged,
     now_hbm,
     adj_hbm,
     prev_hbm,
@@ -455,8 +464,6 @@
 
     for s in range(shots):
         send(halos[0][s])
-    send(adj_halo)
-    send(speed_halo)
 
     def clear(first_field, first_adj, first_border, first_speed, side):
         for k in range(STEPS):
@@ -480,6 +487,8 @@
     across_y[...] = jnp.concatenate([banded(width, width, -43008.0)] * 2, axis=0)
     across_z[...] = jnp.concatenate([banded(group * depth, depth, -42.0)] * 2, axis=1)
 
+    for copy in staged:
+        copy.wait()
     receivers = record_cells.shape[1]
     tiles = receivers // 8
     lane = lax.broadcasted_iota(jnp.int32, (8, width), 1)
@@ -543,6 +552,9 @@
                 (cell == rec_rows).astype(f32).astype(jnp.bfloat16)
             )
 
+        if s == 0:
+            send(adj_halo)
+
     for k in range(STEPS):
         measured[k] = compact[k]
 
@@ -741,14 +753,16 @@
                 forward_point(k, g, (s,))
             if k + 1 < STEPS:
                 send(halos[k + 1][s])
-        for s in everyone:
-            if k == (1 if 2 * s < shots else 2):
-                send(border_halos[s])
         if k == 1:
             sample(0)
             send(samples[0])
         if k + 1 < STEPS:
             forward_inside(k + 1)
+        if k == 0:
+            send(speed_halo)
+        for s in everyone:
+            if k == (1 if 2 * s < shots else 2):
+                send(border_halos[s])
         if k > 0:
             sample(k)
             send(samples[k])
@@ -758,12 +772,13 @@
             prepare(a4, BORDER, ha, BORDER)
             receive(adj_halo)
             sweep(0, groups, free_point, lambda g: mix(ha, g * group + BORDER, blend))
+        else:
+            receive(samples[k - 1])
+            misfits(k - 1, True)
+        if k == 2:
             receive(speed_halo)
             square(0, REACH)
             square(REACH + rows, 2 * REACH + rows)
-        else:
-            receive(samples[k - 1])
-            misfits(k - 1, True)
         if shares and k == 2:
             prior.fold_noise()
     if shares:
@@ -868,7 +883,7 @@
     return pl.pallas_call(
         functools.partial(wave_kernel, doms, shares),
         out_shape=jax.ShapeDtypeStruct(shape, f32),
-        in_specs=[hbm] * 5 + [smem] * 3 + [vmem] * 2 + more_specs,
+        in_specs=[hbm] * 10 + more_specs,
         out_specs=vmem,
         scratch_shapes=first
         + [pltpu.VMEM((shots, rows + 2 * MARGIN, depth, width), f32)] * (STEPS + 1)
@@ -900,6 +915,12 @@
             pltpu.SemaphoreType.DMA((5,)),
             pltpu.SemaphoreType.DMA((exchanges, 2)),
             pltpu.SemaphoreType.DMA((exchanges, 2)),
+            pltpu.SMEM(wavelet.shape, f32),
+            pltpu.SMEM(source_cells.shape, jnp.int32),
+            pltpu.SMEM(signs.shape, jnp.int32),
+            pltpu.VMEM(record_cells.shape, jnp.int32),
+            pltpu.VMEM(observed.shape, f32),
+            pltpu.SemaphoreType.DMA((5,)),
         ]
         + last,
         compiler_params=pltpu.CompilerParams(

time: 55.3 us -> 51.6 us (0.933)
  Pallas kernels: 52.4 us -> 48.7 us
    pallas_call x1, Pallas kernels: 52.4 us -> 48.7 us  [shot_gradient(): pl.pallas_call(functools.partial(wave_kernel, doms, shares), out_shape=ja...]
where the time goes in v5:
time: 51.6 us; the launch traced here: 51.4 us
  Pallas kernels  48.7 us (94%)
  other arithmetic  2.05 us (4%)
  between operations  0.68 us (1%)
    pallas_call x1, Pallas kernels, shot_gradient(): pl.pallas_call(functools.partial(wave_kernel, doms, shares), out_shape=ja...  48.7 us
    add x1, other arithmetic, body(): lax.dynamic_slice_in_dim(velocity, start, shot_rows, 2)  2.05 us

profile of v5, /device:TPU:0, one launch (start us, length us, event | category | flops | bytes accessed | tf_op | source)
XLA Modules:
  0.0 51.4 jit_solution(15734327924419994644)
XLA Ops:
  0.7 0.0 copy-start
  0.7 48.7 %shard_map.136 = f32[1024,128]{1,0:T(8,128)} custom-call(f32[2,32,32,128]{3,2,1,0:T(8,128)} %refs_0_.1, f32[2,32,32,128]{3,2,1,0:T(8,128)} %refs_1_.1, f32[2,32,32,128]{3,2,1,0:T(8,128)} %refs_2_.1, f32[2,32,32,128]{3,2,1,0:T(8,128)} %refs_3_.1, f32[32,32,128]{2,1,0:T(8,128)} %refs_4_.1, f32[2,4]{1,0:T(2,128)} %refs_5_.1, s32[2,8]{1,0:T(2,128)} %refs_6_.1, ...), custom_call_target="tpu_custom_call" | custom-call | tf_op jit(solution)/shard_map/pallas_call | solution.py:883
  49.3 0.0 copy-done
  49.3 2.0 %slice_add_fusion = f32[32,32,32]{2,1,0:T(8,128)} fusion(f32[32,32,128]{2,1,0:T(8,128)} %bitcast.2, f32[32,32,128]{2,1,0:T(8,128)S(1)} %copy-done, s32[]{:T(128)S(6)} %select_n.3), kind=kLoop, calls=%fused_computation | loop fusion | flops 32768 | bytes 393220 | tf_op jit(solution)/shard_map/add | solution.py:1020
Async XLA Ops:
  0.7 48.7 %copy-start = (f32[32,32,128]{2,1,0:T(8,128)S(1)}, f32[32,32,128]{2,1,0:T(8,128)}, u32[]{:S(2)}) copy-start(f32[32,32,128]{2,1,0:T(8,128)} %refs_4_.1) | copy-start | bytes 1572868

commit v6 on v5

--- a/solution.py
+++ b/solution.py
@@ -546,10 +546,13 @@
 
         @pl.loop(0, (rows + 2 * BORDER) // 8)
         def _(c):
-            cell = lax.broadcasted_iota(jnp.int32, (span, receivers), 0)
-            cell = cell + (c * span - BORDER * depth)
-            put[s, pl.ds(pl.multiple_of(c * span, span), span)] = (
-                (cell == rec_rows).astype(f32).astype(jnp.bfloat16)
+            within = lax.broadcasted_iota(jnp.int32, (span, receivers), 0)
+            within = within.astype(f32).astype(jnp.bfloat16)
+            wanted = rec_rows - (c * span - BORDER * depth)
+            wanted = jnp.where((wanted >= 0) & (wanted < span), wanted, -1)
+            wanted = jnp.broadcast_to(wanted.astype(f32).astype(jnp.bfloat16), within.shape)
+            put[s, pl.ds(pl.multiple_of(c * span, span), span)] = jnp.where(
+                within == wanted, jnp.bfloat16(1), jnp.bfloat16(0)
             )
 
         if s == 0:
@@ -813,10 +816,12 @@
         mix(splits[2], g * group + BORDER, blend)
     for g in (-1, groups):
         backward_point(2, g, False)
-    backward(2, 0, groups, True)
+    front = groups // 2 + 2
+    backward(2, 0, front, True)
     backward(1, 0, groups // 2, True)
     if shares:
         prior.share_first(out)
+    backward(2, front, groups, True)
     backward(1, groups // 2, groups, True)
     if shares:
         prior.apply(out)

time: 51.6 us -> 51.2 us (level)
  no operation moved by 1% of the time
where the time goes in v6:
time: 51.2 us; the launch traced here: 51 us
  Pallas kernels  48.3 us (94%)
  other arithmetic  2.05 us (4%)
  between operations  0.68 us (1%)
    pallas_call x1, Pallas kernels, shot_gradient(): pl.pallas_call(functools.partial(wave_kernel, doms, shares), out_shape=ja...  48.3 us
    add x1, other arithmetic, body(): lax.dynamic_slice_in_dim(velocity, start, shot_rows, 2)  2.05 us

profile of v6, /device:TPU:0, one launch (start us, length us, event | category | flops | bytes accessed | tf_op | source)
XLA Modules:
  0.0 51.0 jit_solution(1695000949309103945)
XLA Ops:
  0.7 0.0 copy-start
  0.7 48.3 %shard_map.136 = f32[1024,128]{1,0:T(8,128)} custom-call(f32[2,32,32,128]{3,2,1,0:T(8,128)} %refs_0_.1, f32[2,32,32,128]{3,2,1,0:T(8,128)} %refs_1_.1, f32[2,32,32,128]{3,2,1,0:T(8,128)} %refs_2_.1, f32[2,32,32,128]{3,2,1,0:T(8,128)} %refs_3_.1, f32[32,32,128]{2,1,0:T(8,128)} %refs_4_.1, f32[2,4]{1,0:T(2,128)} %refs_5_.1, s32[2,8]{1,0:T(2,128)} %refs_6_.1, ...), custom_call_target="tpu_custom_call" | custom-call | tf_op jit(solution)/shard_map/pallas_call | solution.py:888
  49.0 0.0 copy-done
  49.0 2.0 %slice_add_fusion = f32[32,32,32]{2,1,0:T(8,128)} fusion(f32[32,32,128]{2,1,0:T(8,128)} %bitcast.2, f32[32,32,128]{2,1,0:T(8,128)S(1)} %copy-done, s32[]{:T(128)S(6)} %select_n.3), kind=kLoop, calls=%fused_computation | loop fusion | flops 32768 | bytes 393220 | tf_op jit(solution)/shard_map/add | solution.py:1025
Async XLA Ops:
  0.7 48.3 %copy-start = (f32[32,32,128]{2,1,0:T(8,128)S(1)}, f32[32,32,128]{2,1,0:T(8,128)}, u32[]{:S(2)}) copy-start(f32[32,32,128]{2,1,0:T(8,128)} %refs_4_.1) | copy-start | bytes 1572868
